TPU v7x, 1024 devices: a whole 8x8x8 slice. The times are simulated.
1024 devices in a mesh: gx: 32 (over y_lo, z), gy: 16 (over x, core), ha: 2 (over y_hi).
Axes of the slice: x: 8, y: 8 (y_hi: 2, y_lo: 4; y = y_hi * 4 + y_lo), z: 8, core: 2. Of those that a mesh axis runs over, the one named last changes fastest.
Arguments:
- offsets: float32 [3, 64, 32, 4, 128], P(None, 'gx', 'gy', 'ha'), may hold values from 0 to 1
- forces: float32 [3, 64, 32, 4, 128], P(None, 'gx', 'gy', 'ha'), may hold values from -6 to 6
- counts: int32 [64, 32, 4], P('gx', 'gy', 'ha'), may hold values from 16 to 128, as said below
Outputs:
- velocity: float32 [3, 64, 32, 4, 128], P(None, 'gx', 'gy', 'ha')
Inputs may be any that keep to these rules, and one draw needn't show every extreme that they name: `counts`: A bin is heavy when its count exceeds 64. The 16 bins that two devices differing only in their ha index hold together include at most 8 heavy bins; in every draw some such pair holds exactly 8, all on one device; some bin holds exactly 128.
All inputs are finite; a program needn't handle non-finite values.
Results may differ from a plain program's by a relative error of at most 0.0003.
Values sent between devices are 32-bit elements; how exact they have to be, the bound alone decides.
A program may use at most 32 MiB of HBM per device.

v0:
```python
import math

import jax
import jax.numpy as jnp
from jax import lax
from jax.sharding import PartitionSpec as P

SPLIT_XI = 2.0
SOFT_SQ = 0.01
GAUSS_COEF = 2.0 * SPLIT_XI / math.sqrt(math.pi)
STOKES_NORM = 1.0 / (8.0 * math.pi)


def padded(array, sides, width):
    for axis, dim in sides:
        size, length = (lax.axis_size(axis), array.shape[dim])
        up = [(i, (i + 1) % size) for i in range(size)]
        down = [(j, i) for i, j in up]
        last = lax.slice_in_dim(array, length - width, length, axis=dim)
        initial = lax.slice_in_dim(array, 0, width, axis=dim)
        before = lax.ppermute(last, axis, up)
        after = lax.ppermute(initial, axis, down)
        array = jnp.concatenate([before, array, after], axis=dim)
    return array


def from_partner(value, axis, stride):
    mask = 2**stride
    pairs = [(source, source ^ mask) for source in range(lax.axis_size(axis))]
    return lax.ppermute(value, axis, pairs)


def pair_kernel(targets, row_ids, source_data, capacity):
    n_source = source_data.shape[1]
    flat_ids = jnp.arange(n_source, dtype=jnp.int32)
    neighbour = flat_ids // capacity
    step_x = (neighbour // 9 - 1).astype(jnp.float32)
    step_y = (neighbour // 3 % 3 - 1).astype(jnp.float32)
    step_z = (neighbour % 3 - 1).astype(jnp.float32)
    delta_x = targets[0][:, None] - (source_data[0] + step_x)[None, :]
    delta_y = targets[1][:, None] - (source_data[1] + step_y)[None, :]
    delta_z = targets[2][:, None] - (source_data[2] + step_z)[None, :]
    square = delta_x * delta_x + delta_y * delta_y + delta_z * delta_z + SOFT_SQ
    radius = jnp.sqrt(square)
    tail_erfc = jax.scipy.special.erfc(SPLIT_XI * radius)
    gaussian = jnp.exp(-SPLIT_XI * SPLIT_XI * square)
    coef_c = tail_erfc / radius + GAUSS_COEF * (2.0 * SPLIT_XI * SPLIT_XI * square - 3.0) * gaussian
    coef_d = (
        tail_erfc / radius + GAUSS_COEF * (1.0 - 2.0 * SPLIT_XI * SPLIT_XI * square) * gaussian
    ) / square
    keep_pair = flat_ids[None, :] != 13 * capacity + row_ids[:, None]
    coef_c = jnp.where(keep_pair, coef_c, 0.0)
    coef_d = jnp.where(keep_pair, coef_d, 0.0)
    force_x = source_data[3][None, :]
    force_y = source_data[4][None, :]
    force_z = source_data[5][None, :]
    along_d = coef_d * (delta_x * force_x + delta_y * force_y + delta_z * force_z)
    vel_x = jnp.sum(coef_c * force_x + along_d * delta_x, axis=1)
    vel_y = jnp.sum(coef_c * force_y + along_d * delta_y, axis=1)
    vel_z = jnp.sum(coef_c * force_z + along_d * delta_z, axis=1)
    return STOKES_NORM * jnp.stack([vel_x, vel_y, vel_z])


def on_device(offsets, forces, counts):
    capacity = offsets.shape[4]
    half_rows = capacity // 2
    size_x = offsets.shape[1]
    size_y = offsets.shape[2]
    size_z = offsets.shape[3]
    n_bins = size_x * size_y * size_z
    n_half = n_bins // 2
    my_index = lax.axis_index("ha")
    slot_ids = jnp.arange(capacity, dtype=jnp.int32)
    live_mask = (slot_ids[None, None, None, :] < counts[..., None]).astype(jnp.float32)
    packed = jnp.concatenate([offsets, forces * live_mask[None]], axis=0)
    extended = padded(packed, (("gx", 1), ("gy", 2), ("ha", 3)), 1)
    padded_cells = jnp.concatenate(
        [extended[:, :, :, -1:], extended, extended[:, :, :, :1]], axis=3
    )
    zero_index = jnp.zeros((), jnp.int32)

    def center_of(flat_id, owner_index):
        bin_x = flat_id // (size_y * size_z)
        bin_y = flat_id // size_z % size_y
        bin_z = flat_id % size_z
        ext_z = (size_z * owner_index + bin_z - size_z * my_index + 1) % (2 * size_z)
        return (bin_x + 1, bin_y + 1, ext_z)

    def fetch_data(center_x, center_y, center_z):
        start_x = center_x - 1
        start_y = center_y - 1
        start_z = jnp.asarray(center_z)
        window = lax.dynamic_slice(
            padded_cells,
            (zero_index, start_x, start_y, start_z, zero_index),
            (6, 3, 3, 3, capacity),
        )
        return window.reshape(6, 27 * capacity)

    def fetch_own(flat_id):
        center_x, center_y, center_z = center_of(flat_id, my_index)
        return fetch_data(center_x, center_y, center_z)

    first_rows = slot_ids[:half_rows]
    second_rows = slot_ids[half_rows:]

    def first_unit(flat_id):
        source_data = fetch_own(flat_id)
        lower = source_data[0:3, 13 * capacity : 13 * capacity + half_rows]
        return pair_kernel(lower, first_rows, source_data, capacity)

    def second_from(source_data):
        upper = source_data[0:3, 13 * capacity + half_rows : 14 * capacity]
        return pair_kernel(upper, second_rows, source_data, capacity)

    bin_ids = jnp.arange(n_bins, dtype=jnp.int32)
    first_part = lax.map(first_unit, bin_ids)
    heavy_flag = (counts.reshape(-1) > half_rows).astype(jnp.int32)
    n_heavy = jnp.sum(heavy_flag)
    ranked = jnp.argsort((1 - heavy_flag) * n_bins + bin_ids)
    placed = jnp.zeros((n_bins, 3, half_rows), jnp.float32)
    kept_ids = ranked[:n_half]
    spare_ids = ranked[n_half:]
    rank_ids = jnp.arange(n_half, dtype=jnp.int32)
    outgoing = lax.map(fetch_own, spare_ids)
    incoming = from_partner(outgoing, "ha", 0)

    def helper_unit(rank_now):
        use_own = rank_now < n_heavy
        far_slot = jnp.clip(rank_now - n_heavy, 0, n_half - 1)
        own_x, own_y, own_z = center_of(kept_ids[rank_now], my_index)
        source_data = jnp.where(use_own, fetch_data(own_x, own_y, own_z), incoming[far_slot])
        return second_from(source_data)

    own_units = lax.map(helper_unit, rank_ids)
    back_ids = jnp.clip(n_heavy + rank_ids, 0, n_half - 1)
    returned = from_partner(own_units[back_ids], "ha", 0)
    kept_valid = (rank_ids < n_heavy).astype(jnp.float32)
    spare_valid = (n_half + rank_ids < n_heavy).astype(jnp.float32)
    placed = placed.at[kept_ids].add(own_units * kept_valid[:, None, None])
    placed = placed.at[spare_ids].add(returned * spare_valid[:, None, None])
    merged = jnp.concatenate([first_part, placed], axis=2)
    result = merged.reshape(size_x, size_y, size_z, 3, capacity).transpose(3, 0, 1, 2, 4)
    return result * live_mask[None]


def solution(mesh):
    in_specs = (
        P(None, "gx", "gy", "ha", None),
        P(None, "gx", "gy", "ha", None),
        P("gx", "gy", "ha"),
    )
    out_specs = P(None, "gx", "gy", "ha", None)
    return jax.shard_map(
        on_device, mesh=mesh, in_specs=in_specs, out_specs=out_specs, check_vma=False
    )
```

profile of v0, /device:TPU:1, one launch (start us, length us, event | category | flops | bytes accessed | tf_op | source)
XLA Modules:
  0.0 184.4 jit_solution(4989300604293205613)
XLA Ops:
  0.0 0.8 compare_convert_fusion
  0.8 0.7 broadcast_multiply_fusion
  1.5 5.7 %collective-permute-start = (f32[6,1,2,2,128]{4,3,2,1,0:T(2,128)S(1)}, f32[6,1,2,2,128]{4,3,2,1,0:T(2,128)S(1)}, u32[]{:S(2)}, u32[]{:S(2)}) collective-permute-start(f32[6,1,2,2,128]{4,3,2,1,0:T(2,128)S(1)} %get-tuple-element.671), channel_id=1, source_target_pairs={{0,32},{32,64},{64,96},{96,128},{128,160},{160,192},{192,224},{224... | collective-permute-start | bytes 36872 | tf_op jit(solution)/shard_map/ppermute | solution.py:21
  7.3 17.4 %collective-permute-start.1 = (f32[6,1,2,2,128]{4,3,2,1,0:T(2,128)S(1)}, f32[6,1,2,2,128]{4,3,2,1,0:T(2,128)S(1)}, u32[]{:S(2)}, u32[]{:S(2)}) collective-permute-start(f32[6,1,2,2,128]{4,3,2,1,0:T(2,128)S(1)} %get-tuple-element.672), channel_id=1, source_target_pairs={{32,0},{64,32},{96,64},{128,96},{160,128},{192,160},{224,192},{256... | collective-permute-start | bytes 36872 | tf_op jit(solution)/shard_map/ppermute | solution.py:22
  25.4 1.0 sort.17
  27.3 2.1 %collective-permute-start.2 = (f32[6,4,1,2,128]{4,3,2,1,0:T(2,128)S(1)}, f32[6,4,1,2,128]{4,3,2,1,0:T(2,128)S(1)}, u32[]{:S(2)}, u32[]{:S(2)}) collective-permute-start(f32[6,4,1,2,128]{4,3,2,1,0:T(2,128)S(1)} %get-tuple-element.669), channel_id=1, source_target_pairs={{0,2},{2,4},{4,6},{6,8},{8,10},{10,12},{12,14},{14,16},{16,18},{18... | collective-permute-start | bytes 73736 | tf_op jit(solution)/shard_map/ppermute | solution.py:21
  30.3 2.3 %collective-permute-done.3 = f32[6,4,1,2,128]{4,3,2,1,0:T(2,128)S(1)} collective-permute-done((f32[6,4,1,2,128]{4,3,2,1,0:T(2,128)S(1)}, f32[6,4,1,2,128]{4,3,2,1,0:T(2,128)S(1)}, u32[]{:S(2)}, u32[]{:S(2)}) %collective-permute-start.3) | collective-permute-done | bytes 24608 | tf_op jit(solution)/shard_map/ppermute | solution.py:22
  32.7 5.2 %collective-permute-start.4 = (f32[6,4,4,1,128]{4,3,2,1,0:T(1,128)S(1)}, f32[6,4,4,1,128]{4,3,2,1,0:T(1,128)S(1)}, u32[]{:S(2)}, u32[]{:S(2)}) collective-permute-start(f32[6,4,4,1,128]{4,3,2,1,0:T(1,128)S(1)} %get-tuple-element.668), channel_id=1, source_target_pairs={{1,0},{0,1},{3,2},{2,3},{5,4},{4,5},{7,6},{6,7},{9,8},{8,9},{11,10... | collective-permute-start | bytes 147464 | tf_op jit(solution)/shard_map/ppermute | solution.py:22
  38.0 4.0 %collective-permute-start.5 = (f32[6,4,4,1,128]{4,3,2,1,0:T(1,128)S(1)}, f32[6,4,4,1,128]{4,3,2,1,0:T(1,128)S(1)}, u32[]{:S(2)}, u32[]{:S(2)}) collective-permute-start(f32[6,4,4,1,128]{4,3,2,1,0:T(1,128)S(1)} %get-tuple-element.667), channel_id=1, source_target_pairs={{0,1},{1,0},{2,3},{3,2},{4,5},{5,4},{6,7},{7,6},{8,9},{9,8},{10,11... | collective-permute-start | bytes 147464 | tf_op jit(solution)/shard_map/ppermute | solution.py:21
  42.7 4.1 %collective-permute-done.5 = f32[6,4,4,1,128]{4,3,2,1,0:T(1,128)S(1)} collective-permute-done((f32[6,4,4,1,128]{4,3,2,1,0:T(1,128)S(1)}, f32[6,4,4,1,128]{4,3,2,1,0:T(1,128)S(1)}, u32[]{:S(2)}, u32[]{:S(2)}) %collective-permute-start.5) | collective-permute-done | bytes 49184 | tf_op jit(solution)/shard_map/ppermute | solution.py:21
  47.2 13.5 %while.50 = (s32[]{:T(128)}, f32[4,6,3456]{2,1,0:T(8,128)S(1)}, s32[4]{0:T(128)S(1)}, f32[6,4,4,6,128]{4,3,2,1,0:T(8,128)S(1)}, s32[]{:T(128)}, /*index=5*/s32[]...) while((s32[]{:T(128)}, f32[4,6,3456]{2,1,0:T(8,128)S(1)}, s32[4]{0:T(128)S(1)}, ...), condition=%wide.region_8.9_spmd, body=%wide.region_7.8_spmd.sunk | while | flops 63 | bytes 553719 | solution.py:125
  47.2 0.7 dynamic_slice.109
  50.6 0.7 dynamic_slice.109
  53.9 0.7 dynamic_slice.109
  57.3 0.7 dynamic_slice.109
  60.7 3.9 %collective-permute-start.6 = (f32[4,6,3456]{2,1,0:T(8,128)S(1)}, f32[4,6,3456]{2,1,0:T(8,128)S(1)}, u32[]{:S(2)}, u32[]{:S(2)}) collective-permute-start(f32[4,6,3456]{2,1,0:T(8,128)S(1)} %get-tuple-element.563), channel_id=1, source_target_pairs={{0,1},{1,0},{2,3},{3,2},{4,5},{5,4},{6,7},{7,6},{8,9},{9,8},{10,11... | collective-permute-start | bytes 995336 | tf_op jit(solution)/shard_map/ppermute | solution.py:30
  64.6 59.9 %while.51 = (s32[]{:T(128)}, f32[8,3,64]{2,1,0:T(4,128)S(1)}, s32[64]{0:T(128)S(1)}, s32[8]{0:T(128)S(1)}, f32[6,4,4,6,128]{4,3,2,1,0:T(8,128)S(1)}, /*index=5*/...) while((s32[]{:T(128)}, f32[8,3,64]{2,1,0:T(4,128)S(1)}, ...), condition=%wide.region_4.5_spmd.clone, body=%wide.region_0.4_spmd.clone.sunk | while | flops 22958724 | bytes 837763 | solution.py:117
  68.2 3.9 %fusion.92 = (f32[64]{0:T(128)S(1)}, f32[64]{0:T(128)S(1)}, f32[64]{0:T(128)S(1)}) fusion(f32[3456]{0:T(1024)S(1)} %mul.1372, f32[3456]{0:T(1024)S(1)} %get-tuple-element.805, f32[64]{0:T(128)S(1)} %get-tuple-element.806, f32[3456]{0:T(1024)S(1)} %fusion.91, f32[64]{0:T(128)S(1)} %get-tuple-element.808, f32[3456]{0:T(1024)S(1)} %get-tuple-element.809, ...), kind=kLoop, calls=%fused_computation.24.clone.1 | loop fusion | flops 22781760 | bytes 84736 | tf_op jit(solution)/shard_map/while/body/eval_jaxpr/reduce_sum | solution.py:58
  75.7 3.9 %fusion.92 = (f32[64]{0:T(128)S(1)}, f32[64]{0:T(128)S(1)}, f32[64]{0:T(128)S(1)}) fusion(f32[3456]{0:T(1024)S(1)} %mul.1372, f32[3456]{0:T(1024)S(1)} %get-tuple-element.805, f32[64]{0:T(128)S(1)} %get-tuple-element.806, f32[3456]{0:T(1024)S(1)} %fusion.91, f32[64]{0:T(128)S(1)} %get-tuple-element.808, f32[3456]{0:T(1024)S(1)} %get-tuple-element.809, ...), kind=kLoop, calls=%fused_computation.24.clone.1 | loop fusion | flops 22781760 | bytes 84736 | tf_op jit(solution)/shard_map/while/body/eval_jaxpr/reduce_sum | solution.py:58
  83.2 3.9 %fusion.92 = (f32[64]{0:T(128)S(1)}, f32[64]{0:T(128)S(1)}, f32[64]{0:T(128)S(1)}) fusion(f32[3456]{0:T(1024)S(1)} %mul.1372, f32[3456]{0:T(1024)S(1)} %get-tuple-element.805, f32[64]{0:T(128)S(1)} %get-tuple-element.806, f32[3456]{0:T(1024)S(1)} %fusion.91, f32[64]{0:T(128)S(1)} %get-tuple-element.808, f32[3456]{0:T(1024)S(1)} %get-tuple-element.809, ...), kind=kLoop, calls=%fused_computation.24.clone.1 | loop fusion | flops 22781760 | bytes 84736 | tf_op jit(solution)/shard_map/while/body/eval_jaxpr/reduce_sum | solution.py:58
  90.7 3.9 %fusion.92 = (f32[64]{0:T(128)S(1)}, f32[64]{0:T(128)S(1)}, f32[64]{0:T(128)S(1)}) fusion(f32[3456]{0:T(1024)S(1)} %mul.1372, f32[3456]{0:T(1024)S(1)} %get-tuple-element.805, f32[64]{0:T(128)S(1)} %get-tuple-element.806, f32[3456]{0:T(1024)S(1)} %fusion.91, f32[64]{0:T(128)S(1)} %get-tuple-element.808, f32[3456]{0:T(1024)S(1)} %get-tuple-element.809, ...), kind=kLoop, calls=%fused_computation.24.clone.1 | loop fusion | flops 22781760 | bytes 84736 | tf_op jit(solution)/shard_map/while/body/eval_jaxpr/reduce_sum | solution.py:58
  98.2 3.9 %fusion.92 = (f32[64]{0:T(128)S(1)}, f32[64]{0:T(128)S(1)}, f32[64]{0:T(128)S(1)}) fusion(f32[3456]{0:T(1024)S(1)} %mul.1372, f32[3456]{0:T(1024)S(1)} %get-tuple-element.805, f32[64]{0:T(128)S(1)} %get-tuple-element.806, f32[3456]{0:T(1024)S(1)} %fusion.91, f32[64]{0:T(128)S(1)} %get-tuple-element.808, f32[3456]{0:T(1024)S(1)} %get-tuple-element.809, ...), kind=kLoop, calls=%fused_computation.24.clone.1 | loop fusion | flops 22781760 | bytes 84736 | tf_op jit(solution)/shard_map/while/body/eval_jaxpr/reduce_sum | solution.py:58
  105.6 3.9 %fusion.92 = (f32[64]{0:T(128)S(1)}, f32[64]{0:T(128)S(1)}, f32[64]{0:T(128)S(1)}) fusion(f32[3456]{0:T(1024)S(1)} %mul.1372, f32[3456]{0:T(1024)S(1)} %get-tuple-element.805, f32[64]{0:T(128)S(1)} %get-tuple-element.806, f32[3456]{0:T(1024)S(1)} %fusion.91, f32[64]{0:T(128)S(1)} %get-tuple-element.808, f32[3456]{0:T(1024)S(1)} %get-tuple-element.809, ...), kind=kLoop, calls=%fused_computation.24.clone.1 | loop fusion | flops 22781760 | bytes 84736 | tf_op jit(solution)/shard_map/while/body/eval_jaxpr/reduce_sum | solution.py:58
  113.1 3.9 %fusion.92 = (f32[64]{0:T(128)S(1)}, f32[64]{0:T(128)S(1)}, f32[64]{0:T(128)S(1)}) fusion(f32[3456]{0:T(1024)S(1)} %mul.1372, f32[3456]{0:T(1024)S(1)} %get-tuple-element.805, f32[64]{0:T(128)S(1)} %get-tuple-element.806, f32[3456]{0:T(1024)S(1)} %fusion.91, f32[64]{0:T(128)S(1)} %get-tuple-element.808, f32[3456]{0:T(1024)S(1)} %get-tuple-element.809, ...), kind=kLoop, calls=%fused_computation.24.clone.1 | loop fusion | flops 22781760 | bytes 84736 | tf_op jit(solution)/shard_map/while/body/eval_jaxpr/reduce_sum | solution.py:58
  120.6 3.9 %fusion.92 = (f32[64]{0:T(128)S(1)}, f32[64]{0:T(128)S(1)}, f32[64]{0:T(128)S(1)}) fusion(f32[3456]{0:T(1024)S(1)} %mul.1372, f32[3456]{0:T(1024)S(1)} %get-tuple-element.805, f32[64]{0:T(128)S(1)} %get-tuple-element.806, f32[3456]{0:T(1024)S(1)} %fusion.91, f32[64]{0:T(128)S(1)} %get-tuple-element.808, f32[3456]{0:T(1024)S(1)} %get-tuple-element.809, ...), kind=kLoop, calls=%fused_computation.24.clone.1 | loop fusion | flops 22781760 | bytes 84736 | tf_op jit(solution)/shard_map/while/body/eval_jaxpr/reduce_sum | solution.py:58
  124.5 49.5 %while.52 = (s32[]{:T(128)}, f32[4,3,64]{2,1,0:T(4,128)S(1)}, s32[64]{0:T(128)S(1)}, s32[4]{0:T(128)S(1)}, s32[]{:T(128)}, /*index=5*/s32[4]{0:T(128)S(1)}, f32[...) while((s32[]{:T(128)}, f32[4,3,64]{2,1,0:T(4,128)S(1)}, ...), condition=%wide.region_13.14_spmd.clone, body=%wide.region_9.13_spmd.clone.sunk | while | flops 22944900 | bytes 837751 | solution.py:135
  133.0 3.9 %fusion.94 = (f32[64]{0:T(128)S(1)}, f32[64]{0:T(128)S(1)}, f32[64]{0:T(128)S(1)}) fusion(f32[3456]{0:T(1024)S(1)} %get-tuple-element.824, f32[3456]{0:T(1024)S(1)} %get-tuple-element.825, f32[64]{0:T(128)S(1)} %get-tuple-element.826, f32[3456]{0:T(1024)S(1)} %get-tuple-element.827, f32[64]{0:T(128)S(1)} %get-tuple-element.828, ...), kind=kLoop, calls=%fused_computation.112.clone.1 | loop fusion | flops 22781760 | bytes 84736 | tf_op jit(solution)/shard_map/while/body/eval_jaxpr/reduce_sum | solution.py:58
  145.4 3.9 %fusion.94 = (f32[64]{0:T(128)S(1)}, f32[64]{0:T(128)S(1)}, f32[64]{0:T(128)S(1)}) fusion(f32[3456]{0:T(1024)S(1)} %get-tuple-element.824, f32[3456]{0:T(1024)S(1)} %get-tuple-element.825, f32[64]{0:T(128)S(1)} %get-tuple-element.826, f32[3456]{0:T(1024)S(1)} %get-tuple-element.827, f32[64]{0:T(128)S(1)} %get-tuple-element.828, ...), kind=kLoop, calls=%fused_computation.112.clone.1 | loop fusion | flops 22781760 | bytes 84736 | tf_op jit(solution)/shard_map/while/body/eval_jaxpr/reduce_sum | solution.py:58
  157.8 3.9 %fusion.94 = (f32[64]{0:T(128)S(1)}, f32[64]{0:T(128)S(1)}, f32[64]{0:T(128)S(1)}) fusion(f32[3456]{0:T(1024)S(1)} %get-tuple-element.824, f32[3456]{0:T(1024)S(1)} %get-tuple-element.825, f32[64]{0:T(128)S(1)} %get-tuple-element.826, f32[3456]{0:T(1024)S(1)} %get-tuple-element.827, f32[64]{0:T(128)S(1)} %get-tuple-element.828, ...), kind=kLoop, calls=%fused_computation.112.clone.1 | loop fusion | flops 22781760 | bytes 84736 | tf_op jit(solution)/shard_map/while/body/eval_jaxpr/reduce_sum | solution.py:58
  170.2 3.9 %fusion.94 = (f32[64]{0:T(128)S(1)}, f32[64]{0:T(128)S(1)}, f32[64]{0:T(128)S(1)}) fusion(f32[3456]{0:T(1024)S(1)} %get-tuple-element.824, f32[3456]{0:T(1024)S(1)} %get-tuple-element.825, f32[64]{0:T(128)S(1)} %get-tuple-element.826, f32[3456]{0:T(1024)S(1)} %get-tuple-element.827, f32[64]{0:T(128)S(1)} %get-tuple-element.828, ...), kind=kLoop, calls=%fused_computation.112.clone.1 | loop fusion | flops 22781760 | bytes 84736 | tf_op jit(solution)/shard_map/while/body/eval_jaxpr/reduce_sum | solution.py:58
  174.7 5.3 %collective-permute-start.7 = (f32[4,3,64]{2,1,0:T(4,128)S(1)}, f32[4,3,64]{2,1,0:T(4,128)S(1)}, u32[]{:S(2)}, u32[]{:S(2)}) collective-permute-start(f32[4,3,64]{2,1,0:T(4,128)S(1)} %gather_fusion), channel_id=1, source_target_pairs={{0,1},{1,0},{2,3},{3,2},{4,5},{5,4},{6,7},{7,6},{8,9},{9,8},{10,11... | collective-permute-start | bytes 9224 | tf_op jit(solution)/shard_map/ppermute | solution.py:30
  180.7 2.3 %collective-permute-done.7 = f32[4,3,64]{2,1,0:T(4,128)S(1)} collective-permute-done((f32[4,3,64]{2,1,0:T(4,128)S(1)}, f32[4,3,64]{2,1,0:T(4,128)S(1)}, u32[]{:S(2)}, u32[]{:S(2)}) %collective-permute-start.7) | collective-permute-done | bytes 3104 | tf_op jit(solution)/shard_map/ppermute | solution.py:30
  (210 shorter events, 20.8 us)
Async XLA Ops:
  0.8 0.7 copy-start
  1.5 23.2 %copy-start.1 = (s32[2,2,2]{2,1,0:T(2,128)S(1)}, s32[2,2,2]{2,1,0:T(2,128)}, u32[]{:S(2)}) copy-start(s32[2,2,2]{2,1,0:T(2,128)} %param.11) | copy-start | bytes 100
  1.5 25.7 %collective-permute-start = (f32[6,1,2,2,128]{4,3,2,1,0:T(2,128)S(1)}, f32[6,1,2,2,128]{4,3,2,1,0:T(2,128)S(1)}, u32[]{:S(2)}, u32[]{:S(2)}) collective-permute-start(f32[6,1,2,2,128]{4,3,2,1,0:T(2,128)S(1)} %get-tuple-element.671), channel_id=1, source_target_pairs={{0,32},{32,64},{64,96},{96,128},{128,160},{160,192},{192,224},{224... | collective-permute-start | bytes 36872 | tf_op jit(solution)/shard_map/ppermute | solution.py:21
  7.3 20.0 %collective-permute-start.1 = (f32[6,1,2,2,128]{4,3,2,1,0:T(2,128)S(1)}, f32[6,1,2,2,128]{4,3,2,1,0:T(2,128)S(1)}, u32[]{:S(2)}, u32[]{:S(2)}) collective-permute-start(f32[6,1,2,2,128]{4,3,2,1,0:T(2,128)S(1)} %get-tuple-element.672), channel_id=1, source_target_pairs={{32,0},{64,32},{96,64},{128,96},{160,128},{192,160},{224,192},{256... | collective-permute-start | bytes 36872 | tf_op jit(solution)/shard_map/ppermute | solution.py:22
  27.3 3.0 %collective-permute-start.2 = (f32[6,4,1,2,128]{4,3,2,1,0:T(2,128)S(1)}, f32[6,4,1,2,128]{4,3,2,1,0:T(2,128)S(1)}, u32[]{:S(2)}, u32[]{:S(2)}) collective-permute-start(f32[6,4,1,2,128]{4,3,2,1,0:T(2,128)S(1)} %get-tuple-element.669), channel_id=1, source_target_pairs={{0,2},{2,4},{4,6},{6,8},{8,10},{10,12},{12,14},{14,16},{16,18},{18... | collective-permute-start | bytes 73736 | tf_op jit(solution)/shard_map/ppermute | solution.py:21
  29.4 3.3 %collective-permute-start.3 = (f32[6,4,1,2,128]{4,3,2,1,0:T(2,128)S(1)}, f32[6,4,1,2,128]{4,3,2,1,0:T(2,128)S(1)}, u32[]{:S(2)}, u32[]{:S(2)}) collective-permute-start(f32[6,4,1,2,128]{4,3,2,1,0:T(2,128)S(1)} %get-tuple-element.670), channel_id=1, source_target_pairs={{2,0},{4,2},{6,4},{8,6},{10,8},{12,10},{14,12},{16,14},{18,16},{20... | collective-permute-start | bytes 73736 | tf_op jit(solution)/shard_map/ppermute | solution.py:22
  32.7 10.0 %collective-permute-start.4 = (f32[6,4,4,1,128]{4,3,2,1,0:T(1,128)S(1)}, f32[6,4,4,1,128]{4,3,2,1,0:T(1,128)S(1)}, u32[]{:S(2)}, u32[]{:S(2)}) collective-permute-start(f32[6,4,4,1,128]{4,3,2,1,0:T(1,128)S(1)} %get-tuple-element.668), channel_id=1, source_target_pairs={{1,0},{0,1},{3,2},{2,3},{5,4},{4,5},{7,6},{6,7},{9,8},{8,9},{11,10... | collective-permute-start | bytes 147464 | tf_op jit(solution)/shard_map/ppermute | solution.py:22
  38.0 8.8 %collective-permute-start.5 = (f32[6,4,4,1,128]{4,3,2,1,0:T(1,128)S(1)}, f32[6,4,4,1,128]{4,3,2,1,0:T(1,128)S(1)}, u32[]{:S(2)}, u32[]{:S(2)}) collective-permute-start(f32[6,4,4,1,128]{4,3,2,1,0:T(1,128)S(1)} %get-tuple-element.667), channel_id=1, source_target_pairs={{0,1},{1,0},{2,3},{3,2},{4,5},{5,4},{6,7},{7,6},{8,9},{9,8},{10,11... | collective-permute-start | bytes 147464 | tf_op jit(solution)/shard_map/ppermute | solution.py:21
  60.7 63.9 %collective-permute-start.6 = (f32[4,6,3456]{2,1,0:T(8,128)S(1)}, f32[4,6,3456]{2,1,0:T(8,128)S(1)}, u32[]{:S(2)}, u32[]{:S(2)}) collective-permute-start(f32[4,6,3456]{2,1,0:T(8,128)S(1)} %get-tuple-element.563), channel_id=1, source_target_pairs={{0,1},{1,0},{2,3},{3,2},{4,5},{5,4},{6,7},{7,6},{8,9},{9,8},{10,11... | collective-permute-start | bytes 995336 | tf_op jit(solution)/shard_map/ppermute | solution.py:30
  174.7 8.3 %collective-permute-start.7 = (f32[4,3,64]{2,1,0:T(4,128)S(1)}, f32[4,3,64]{2,1,0:T(4,128)S(1)}, u32[]{:S(2)}, u32[]{:S(2)}) collective-permute-start(f32[4,3,64]{2,1,0:T(4,128)S(1)} %gather_fusion), channel_id=1, source_target_pairs={{0,1},{1,0},{2,3},{3,2},{4,5},{5,4},{6,7},{7,6},{8,9},{9,8},{10,11... | collective-permute-start | bytes 9224 | tf_op jit(solution)/shard_map/ppermute | solution.py:30
where the time goes:
time: 188 us; the launch traced here: 184 us
  loops' own time  59.3 us (32%)
  other arithmetic  56.2 us (30%)
  starting transfers between devices  43.6 us (23%)
  local copies, waits for them, and re-layouts  16.1 us (9%)
  waiting for transfers between devices  8.95 us (5%)
    reduce_sum x12, other arithmetic, pair_kernel(): vel_x = jnp.sum(coef_c * force_x + along_d * delta_x, axis=1)  46.6 us
    another operation x1, loops' own time, on_device(): own_units = lax.map(helper_unit, rank_ids)  27 us
    ppermute x3, starting transfers between devices, padded(): after = lax.ppermute(initial, axis, down)  22.6 us
    another operation x1, loops' own time, on_device(): first_part = lax.map(first_unit, bin_ids)  21.7 us
    ppermute x3, starting transfers between devices, padded(): before = lax.ppermute(last, axis, up)  11.8 us
    another operation x1, loops' own time, on_device(): outgoing = lax.map(fetch_own, spare_ids)  10.6 us
    ppermute x2, starting transfers between devices, from_partner(): return lax.ppermute(value, axis, pairs)  9.18 us
    dynamic_slice x8, local copies, waits for them, and re-layouts, on_device(): outgoing = lax.map(fetch_own, spare_ids)  4.93 us
  transfers between devices with their start and end apart: 8, of which 4 were waited for; matrix products, arithmetic and copies ran while one was open for 23% of the time, Pallas kernels for 0%

commit v1 on v0

v1 whole, which is shorter than its diff:
```python
import math

import jax
import jax.numpy as jnp
from jax import lax
from jax.experimental import pallas as pl
from jax.experimental.pallas import tpu as pltpu
from jax.sharding import PartitionSpec as P


GAUSS = 4.0 / math.sqrt(math.pi)
NORM = 1.0 / (8.0 * math.pi)
ERFCX = (-6.605853591129529e-05, 0.2835500330769051, 0.2685154202156198, 0.31675806246707194,
         -0.03963002369445217, 0.48597127806071433, -0.4204782835714706, 0.1053890269858883)
UNIT = 32
BATCH = 8
F32 = jnp.float32
BF16 = jnp.bfloat16


def split3(v):
    a = v.astype(BF16).astype(F32)
    r = v - a
    b = r.astype(BF16).astype(F32)
    return a, b, r - b


def coefs(sq, keep=None):
    rs = lax.rsqrt(sq)
    rad = sq * rs
    z = rad + 1.0
    t = lax.rsqrt(z * z)
    p = ERFCX[7]
    for q in ERFCX[6::-1]:
        p = p * t + q
    e = rs * p
    g = jnp.exp(-4.0 * sq)
    if keep is not None:
        g = jnp.where(keep, g, 0.0)
    a = (8.0 * GAUSS) * sq
    c = g * ((e - 3.0 * GAUSS) + a)
    d = (g * (rs * rs)) * ((e + GAUSS) - a)
    ch = c.astype(BF16)
    cl = (c - ch.astype(F32)).astype(BF16)
    dh = d.astype(BF16)
    dl = (d - dh.astype(F32)).astype(BF16)
    return ch, cl, dh, dl


def near_kernel(reg_ref, out_ref, fa, qf, a_ref, q_ref, b_ref, cc, cd, nq_v, nq_s, lst, sem):
    off = [reg_ref[:, r, :] for r in range(3)]
    frc = [reg_ref[:, 3 + r, :] for r in range(3)]
    cnt = reg_ref[:, 6, :]
    nq = jnp.where(cnt > 32.0, 1, 0) + jnp.where(cnt > 64.0, 1, 0) + jnp.where(cnt > 96.0, 1, 0) + 1
    nq_v[...] = nq.astype(jnp.int32)
    cp = pltpu.make_async_copy(nq_v, nq_s, sem)
    cp.start()
    bid = lax.broadcasted_iota(jnp.int32, (64, 128), 0)
    xi = bid // 16
    yi = (bid // 4) % 4
    zi = bid % 4
    zc = jnp.where(zi == 3, -2, zi - 1)
    pos = [off[0] + (xi - 2).astype(F32), off[1] + (yi - 2).astype(F32), off[2] + zc.astype(F32)]
    nrm = pos[0] * pos[0] + pos[1] * pos[1] + pos[2] * pos[2]
    for a in range(3):
        p = split3(-2.0 * pos[a])
        for i, k in enumerate((0, 0, 0, 1, 1, 2)):
            fa[6 * a + i] = p[k]
    one = jnp.ones((64, 128), F32)
    for i in range(3):
        fa[18 + i] = one
    n3 = split3(nrm)
    for i in range(3):
        fa[21 + i] = n3[i]
    for i in range(24, 32):
        fa[i] = jnp.zeros((64, 128), F32)
    for b in range(3):
        s = split3(frc[b])
        for k in range(3):
            qf[3 * k + b] = s[k]
    for i in range(9, 16):
        qf[i] = jnp.zeros((64, 128), F32)
    w = pos[0] * frc[0] + pos[1] * frc[1] + pos[2] * frc[2]
    qs = frc + [w] + [frc[b] * pos[a] for a in range(3) for b in range(3)] + [w * pos[a] for a in range(3)]
    for i, v in enumerate(qs):
        s = split3(v)
        for k in range(3):
            qf[16 + 16 * k + i] = s[k]

    @pl.loop(0, 64, unroll=4)
    def _(b):
        q = qf[:, b, :].astype(BF16)
        q_ref[b, :, 0:128] = q
        q_ref[b, :, 128:256] = q
        at = fa[:, b, :].T.astype(BF16)
        for u in range(4):
            a_ref[4 * b + u] = at[32 * u:32 * (u + 1)]

    cc[...] = jnp.zeros_like(cc)
    cd[...] = jnp.zeros_like(cd)
    cp.wait()
    rowi = lax.broadcasted_iota(jnp.int32, (128, 128), 0)
    lani = lax.broadcasted_iota(jnp.int32, (128, 128), 1)

    @pl.loop(0, 8)
    def _(o):
        xo = o // 4
        yo = (o // 2) % 2
        ko = o % 2
        ob = (xo + 1) * 16 + (yo + 1) * 4 + ko
        T = reg_ref[ob]
        x = T[0:1] + (xo - 1).astype(F32)
        y = T[1:2] + (yo - 1).astype(F32)
        z = T[2:3] + (ko - 1).astype(F32)
        tp = [x, y, z]
        m3 = split3(x * x + y * y + z * z + 0.01)
        o1 = jnp.ones((1, 128), F32)
        rows = []
        for a in range(3):
            s = split3(tp[a])
            rows += [s[0], s[1], s[2], s[0], s[1], s[0]]
        rows += [m3[0], m3[1], m3[2], o1, o1, o1]
        rows += [jnp.zeros((8, 128), F32)]
        bmat = jnp.concatenate(rows, axis=0).astype(BF16)
        n = jnp.int32(0)
        for j in range(27):
            if j == 13:
                continue
            b = (xo + j // 9) * 16 + (yo + (j // 3) % 3) * 4 + (ko + j % 3 + 3) % 4
            e = b * 512 + j * 4
            for u in range(4):
                lst[n + u] = e * 1 + u * 129
            n = n + nq_s[b, 0]
        for u in range(BATCH):
            lst[n + u] = lst[0]

        aown = jnp.concatenate([a_ref[4 * ob + u] for u in range(4)], axis=0)
        sq = jnp.dot(aown, bmat, preferred_element_type=F32)
        ch, cl, dh, dl = coefs(sq, rowi != lani)
        cc[13, 0:128] = ch
        cc[13, 128:256] = cl
        cd[13, 0:128] = dh
        cd[13, 128:256] = dl

        @pl.loop(0, (n + BATCH - 1) // BATCH)
        def _(it):
            gs = []
            js = []
            for u in range(BATCH):
                v = lst[it * BATCH + u]
                gs.append(v // 128)
                js.append(v % 128)
            am = jnp.concatenate([a_ref[g] for g in gs], axis=0)
            sq = jnp.dot(am, bmat, preferred_element_type=F32)
            ch, cl, dh, dl = coefs(sq)
            for u in range(BATCH):
                j = js[u] // 4
                r = pl.multiple_of((js[u] % 4) * 32, 32)
                s = slice(32 * u, 32 * (u + 1))
                cc[j, pl.ds(r, 32)] = ch[s]
                cc[j, pl.ds(r + 128, 32)] = cl[s]
                cd[j, pl.ds(r, 32)] = dh[s]
                cd[j, pl.ds(r + 128, 32)] = dl[s]

        ac = jnp.zeros((16, 128), F32)
        ad = jnp.zeros((48, 128), F32)
        for j in range(27):
            b = (xo + j // 9) * 16 + (yo + (j // 3) % 3) * 4 + (ko + j % 3 + 3) % 4
            ac = ac + jnp.dot(q_ref[b, 0:16], cc[j], preferred_element_type=F32)
            ad = ad + jnp.dot(q_ref[b, 16:64], cd[j], preferred_element_type=F32)
        cv = (ac[6:9] + ac[3:6]) + ac[0:3]
        dq = (ad[32:48] + ad[16:32]) + ad[0:16]
        live = (lax.broadcasted_iota(jnp.int32, (1, 128), 1).astype(F32) < T[6:7]).astype(F32) * NORM
        xf = (x * dq[0:1] + y * dq[1:2] + z * dq[2:3]) - dq[3:4]
        for a in range(3):
            v = cv[a:a + 1] + tp[a] * xf
            i = 4 + 3 * a
            v = v - ((x * dq[i:i + 1] + y * dq[i + 1:i + 2] + z * dq[i + 2:i + 3]) - dq[13 + a:14 + a])
            out_ref[a, pl.ds(o, 1)] = v * live


def near_call(region):
    return pl.pallas_call(
        near_kernel,
        out_shape=jax.ShapeDtypeStruct((3, 8, 128), F32),
        in_specs=[pl.BlockSpec(memory_space=pltpu.VMEM)],
        out_specs=pl.BlockSpec(memory_space=pltpu.VMEM),
        scratch_shapes=[
            pltpu.VMEM((32, 64, 128), F32),
            pltpu.VMEM((64, 64, 128), F32),
            pltpu.VMEM((256, 32, 32), BF16),
            pltpu.VMEM((64, 64, 256), BF16),
            pltpu.VMEM((32, 128), BF16),
            pltpu.VMEM((27, 256, 128), BF16),
            pltpu.VMEM((27, 256, 128), BF16),
            pltpu.VMEM((64, 128), jnp.int32),
            pltpu.SMEM((64, 128), jnp.int32),
            pltpu.SMEM((160,), jnp.int32),
            pltpu.SemaphoreType.DMA,
        ],
    )(region)


def halo(array, axis, dim):
    n = lax.axis_size(axis)
    up = [(i, (i + 1) % n) for i in range(n)]
    down = [(j, i) for i, j in up]
    last = lax.slice_in_dim(array, 1, 2, axis=dim)
    first = lax.slice_in_dim(array, 0, 1, axis=dim)
    before = lax.ppermute(last, axis, up)
    after = lax.ppermute(first, axis, down)
    return jnp.concatenate([before, array, after], axis=dim)


def on_device(offsets, forces, counts):
    slots = jnp.arange(128, dtype=jnp.int32)
    live = (slots < counts[..., None]).astype(F32)
    rows = jnp.concatenate([offsets, forces * live[None]], axis=0).transpose(1, 2, 3, 0, 4)
    cnt = jnp.broadcast_to(counts.astype(F32)[..., None, None], (2, 2, 2, 2, 128))
    packed = jnp.concatenate([rows, cnt], axis=3)
    ext = halo(halo(packed, "gx", 0), "gy", 1)
    other = lax.ppermute(ext, "ha", [(0, 1), (1, 0)])
    region = jnp.concatenate([ext, other], axis=2).reshape(64, 8, 128)
    return near_call(region).reshape(3, 2, 2, 2, 128)


def solution(mesh):
    spec = P(None, "gx", "gy", "ha", None)
    return jax.shard_map(
        on_device, mesh=mesh, in_specs=(spec, spec, P("gx", "gy", "ha")), out_specs=spec, check_vma=False
    )
```

time: 188 us -> 82 us (0.44); the launches traced: 184 us -> 81.7 us
  loops' own time: 59.3 us -> 0 us
  other arithmetic: 56.2 us -> 1.79 us
  Pallas kernels: 0 us -> 35.4 us
  local copies, waits for them, and re-layouts: 16.1 us -> 0.95 us
  starting transfers between devices: 43.6 us -> 31 us
  waiting for transfers between devices: 8.95 us -> 12.5 us
    another operation x3 -> x0, loops' own time: 59.3 us -> none  [the longest x1 27 us: on_device(): own_units = lax.map(helper_unit, rank_ids)]
    reduce_sum x13 -> x0, other arithmetic: 47.3 us -> none  [the longest x12 46.6 us: pair_kernel(): vel_x = jnp.sum(coef_c * force_x + along_d * delta_x, axis=1)]
    pallas_call x0 -> x1, Pallas kernels: none -> 35.4 us  [near_call(): pl.pallas_call(near_kernel, out_shape=jax.ShapeDtypeStruct((3, 8, 128), F...]
    dynamic_slice x40 -> x0, local copies, waits for them, and re-layouts: 13 us -> none  [the longest x8 4.93 us: on_device(): outgoing = lax.map(fetch_own, spare_ids)]
    ppermute x8 -> x5, starting transfers between devices: 43.6 us -> 31 us  [the longest x2 17.4 us: halo(): after = lax.ppermute(first, axis, down)]
    ppermute x8 -> x5, waiting for transfers between devices: 8.95 us -> 12.5 us  [the longest x1 8.35 us: on_device(): other = lax.ppermute(ext, 'ha', [(0, 1), (1, 0)])]
  transfers between devices with their start and end apart: 8 -> 5, of which waited for: 4 -> 4; matrix products, arithmetic and copies ran while one was open for 23% -> 0% of each run, Pallas kernels for 0% -> 0%
where the time goes in v1:
time: 82 us; the launch traced here: 81.7 us
  Pallas kernels  35.4 us (43%)
  starting transfers between devices  31 us (38%)
  waiting for transfers between devices  12.5 us (15%)
  other arithmetic  1.79 us (2%)
  local copies, waits for them, and re-layouts  0.95 us (1%)
    pallas_call x1, Pallas kernels, near_call(): pl.pallas_call(near_kernel, out_shape=jax.ShapeDtypeStruct((3, 8, 128), F...  35.4 us
    ppermute x2, starting transfers between devices, halo(): after = lax.ppermute(first, axis, down)  17.4 us
    ppermute x2, starting transfers between devices, halo(): before = lax.ppermute(last, axis, up)  8.38 us
    ppermute x1, waiting for transfers between devices, on_device(): other = lax.ppermute(ext, 'ha', [(0, 1), (1, 0)])  8.35 us
    ppermute x1, starting transfers between devices, on_device(): other = lax.ppermute(ext, 'ha', [(0, 1), (1, 0)])  5.21 us
    ppermute x2, waiting for transfers between devices, halo(): after = lax.ppermute(first, axis, down)  3.15 us
  transfers between devices with their start and end apart: 5, of which 4 were waited for; matrix products, arithmetic and copies ran while one was open for 0% of the time, Pallas kernels for 0%

profile of v1, /device:TPU:1, one launch (start us, length us, event | category | flops | bytes accessed | tf_op | source)
XLA Modules:
  0.0 81.7 jit_solution(18096633627539498602)
XLA Ops:
  0.0 0.0 copy-start.1
  0.0 0.8 convert_element_type.11
  0.8 0.0 copy-done.1
  0.8 0.1 compare_convert_fusion
  0.8 0.0 copy-start
  0.8 0.7 broadcast_multiply_fusion
  1.6 0.0 copy-done
  1.6 0.1 broadcast_in_dim.2
  1.7 5.7 %collective-permute-start = (f32[1,2,2,8,128]{4,2,1,0,3:T(2,128)S(1)}, f32[1,2,2,8,128]{4,2,1,0,3:T(2,128)S(1)}, u32[]{:S(2)}, u32[]{:S(2)}) collective-permute-start(f32[1,2,2,8,128]{4,2,1,0,3:T(2,128)S(1)} %get-tuple-element.7), channel_id=1, source_target_pairs={{0,32},{32,64},{64,96},{96,128},{128,160},{160,192},{192,224},{224... | collective-permute-start | bytes 49160 | tf_op jit(solution)/shard_map/ppermute | solution.py:210
  7.4 17.4 %collective-permute-start.1 = (f32[1,2,2,8,128]{4,2,1,0,3:T(2,128)S(1)}, f32[1,2,2,8,128]{4,2,1,0,3:T(2,128)S(1)}, u32[]{:S(2)}, u32[]{:S(2)}) collective-permute-start(f32[1,2,2,8,128]{4,2,1,0,3:T(2,128)S(1)} %get-tuple-element.8), channel_id=1, source_target_pairs={{32,0},{64,32},{96,64},{128,96},{160,128},{192,160},{224,192},{256... | collective-permute-start | bytes 49160 | tf_op jit(solution)/shard_map/ppermute | solution.py:211
  24.9 0.0 collective-permute-done
  24.9 0.8 %collective-permute-done.1 = f32[1,2,2,8,128]{4,2,1,0,3:T(2,128)S(1)} collective-permute-done((f32[1,2,2,8,128]{4,2,1,0,3:T(2,128)S(1)}, f32[1,2,2,8,128]{4,2,1,0,3:T(2,128)S(1)}, u32[]{:S(2)}, u32[]{:S(2)}) %collective-permute-start.1) | collective-permute-done | bytes 16416 | tf_op jit(solution)/shard_map/ppermute | solution.py:211
  25.8 2.6 %collective-permute-start.2 = (f32[4,1,2,8,128]{4,2,1,0,3:T(2,128)S(1)}, f32[4,1,2,8,128]{4,2,1,0,3:T(2,128)S(1)}, u32[]{:S(2)}, u32[]{:S(2)}) collective-permute-start(f32[4,1,2,8,128]{4,2,1,0,3:T(2,128)S(1)} %get-tuple-element.5), channel_id=1, source_target_pairs={{0,2},{2,4},{4,6},{6,8},{8,10},{10,12},{12,14},{14,16},{16,18},{18... | collective-permute-start | bytes 98312 | tf_op jit(solution)/shard_map/ppermute | solution.py:210
  28.4 0.0 collective-permute-start.3
  28.4 1.0 %collective-permute-done.2 = f32[4,1,2,8,128]{4,2,1,0,3:T(2,128)S(1)} collective-permute-done((f32[4,1,2,8,128]{4,2,1,0,3:T(2,128)S(1)}, f32[4,1,2,8,128]{4,2,1,0,3:T(2,128)S(1)}, u32[]{:S(2)}, u32[]{:S(2)}) %collective-permute-start.2) | collective-permute-done | bytes 32800 | tf_op jit(solution)/shard_map/ppermute | solution.py:210
  29.4 2.3 %collective-permute-done.3 = f32[4,1,2,8,128]{4,2,1,0,3:T(2,128)S(1)} collective-permute-done((f32[4,1,2,8,128]{4,2,1,0,3:T(2,128)S(1)}, f32[4,1,2,8,128]{4,2,1,0,3:T(2,128)S(1)}, u32[]{:S(2)}, u32[]{:S(2)}) %collective-permute-start.3) | collective-permute-done | bytes 32800 | tf_op jit(solution)/shard_map/ppermute | solution.py:211
  31.7 0.1 pad_maximum_fusion.1
  31.8 5.2 %collective-permute-start.4 = (f32[4,4,2,8,128]{4,2,1,0,3:T(2,128)S(1)}, f32[4,4,2,8,128]{4,2,1,0,3:T(2,128)S(1)}, u32[]{:S(2)}, u32[]{:S(2)}) collective-permute-start(f32[4,4,2,8,128]{4,2,1,0,3:T(2,128)S(1)} %pad_maximum_fusion.1), channel_id=1, source_target_pairs={{0,1},{1,0},{2,3},{3,2},{4,5},{5,4},{6,7},{7,6},{8,9},{9,8},{10,11... | collective-permute-start | bytes 393224 | tf_op jit(solution)/shard_map/ppermute | solution.py:222
  37.0 8.4 %collective-permute-done.4 = f32[4,4,2,8,128]{4,2,1,0,3:T(2,128)S(1)} collective-permute-done((f32[4,4,2,8,128]{4,2,1,0,3:T(2,128)S(1)}, f32[4,4,2,8,128]{4,2,1,0,3:T(2,128)S(1)}, u32[]{:S(2)}, u32[]{:S(2)}) %collective-permute-start.4) | collective-permute-done | bytes 131104 | tf_op jit(solution)/shard_map/ppermute | solution.py:222
  45.4 0.1 pad_maximum_fusion
  45.5 0.8 %copy.4 = f32[4,4,4,8,128]{4,3,2,1,0:T(8,128)} copy(f32[4,4,4,8,128]{4,2,1,0,3:T(4,128)S(1)} %pad_maximum_fusion) | data formatting | bytes 524288 | tf_op jit(solution)/shard_map/concatenate | solution.py:223
  46.4 35.4 %shard_map.37 = f32[3,8,128]{2,1,0:T(8,128)} custom-call(f32[64,8,128]{2,1,0:T(8,128)} %bitcast.4), custom_call_target="tpu_custom_call" | custom-call | tf_op jit(solution)/shard_map/pallas_call | solution.py:183
  (4 shorter events, 0.1 us)
Async XLA Ops:
  0.0 0.8 copy-start.1
  0.8 0.7 copy-start
  1.7 23.2 %collective-permute-start = (f32[1,2,2,8,128]{4,2,1,0,3:T(2,128)S(1)}, f32[1,2,2,8,128]{4,2,1,0,3:T(2,128)S(1)}, u32[]{:S(2)}, u32[]{:S(2)}) collective-permute-start(f32[1,2,2,8,128]{4,2,1,0,3:T(2,128)S(1)} %get-tuple-element.7), channel_id=1, source_target_pairs={{0,32},{32,64},{64,96},{96,128},{128,160},{160,192},{192,224},{224... | collective-permute-start | bytes 49160 | tf_op jit(solution)/shard_map/ppermute | solution.py:210
  7.4 18.3 %collective-permute-start.1 = (f32[1,2,2,8,128]{4,2,1,0,3:T(2,128)S(1)}, f32[1,2,2,8,128]{4,2,1,0,3:T(2,128)S(1)}, u32[]{:S(2)}, u32[]{:S(2)}) collective-permute-start(f32[1,2,2,8,128]{4,2,1,0,3:T(2,128)S(1)} %get-tuple-element.8), channel_id=1, source_target_pairs={{32,0},{64,32},{96,64},{128,96},{160,128},{192,160},{224,192},{256... | collective-permute-start | bytes 49160 | tf_op jit(solution)/shard_map/ppermute | solution.py:211
  25.8 3.7 %collective-permute-start.2 = (f32[4,1,2,8,128]{4,2,1,0,3:T(2,128)S(1)}, f32[4,1,2,8,128]{4,2,1,0,3:T(2,128)S(1)}, u32[]{:S(2)}, u32[]{:S(2)}) collective-permute-start(f32[4,1,2,8,128]{4,2,1,0,3:T(2,128)S(1)} %get-tuple-element.5), channel_id=1, source_target_pairs={{0,2},{2,4},{4,6},{6,8},{8,10},{10,12},{12,14},{14,16},{16,18},{18... | collective-permute-start | bytes 98312 | tf_op jit(solution)/shard_map/ppermute | solution.py:210
  28.4 3.3 %collective-permute-start.3 = (f32[4,1,2,8,128]{4,2,1,0,3:T(2,128)S(1)}, f32[4,1,2,8,128]{4,2,1,0,3:T(2,128)S(1)}, u32[]{:S(2)}, u32[]{:S(2)}) collective-permute-start(f32[4,1,2,8,128]{4,2,1,0,3:T(2,128)S(1)} %get-tuple-element.6), channel_id=1, source_target_pairs={{2,0},{4,2},{6,4},{8,6},{10,8},{12,10},{14,12},{16,14},{18,16},{20... | collective-permute-start | bytes 98312 | tf_op jit(solution)/shard_map/ppermute | solution.py:211
  31.8 13.6 %collective-permute-start.4 = (f32[4,4,2,8,128]{4,2,1,0,3:T(2,128)S(1)}, f32[4,4,2,8,128]{4,2,1,0,3:T(2,128)S(1)}, u32[]{:S(2)}, u32[]{:S(2)}) collective-permute-start(f32[4,4,2,8,128]{4,2,1,0,3:T(2,128)S(1)} %pad_maximum_fusion.1), channel_id=1, source_target_pairs={{0,1},{1,0},{2,3},{3,2},{4,5},{5,4},{6,7},{7,6},{8,9},{9,8},{10,11... | collective-permute-start | bytes 393224 | tf_op jit(solution)/shard_map/ppermute | solution.py:222

commit v2 on v1

--- a/solution.py
+++ b/solution.py
@@ -48,9 +48,9 @@
 
 
 def near_kernel(reg_ref, out_ref, fa, qf, a_ref, q_ref, b_ref, cc, cd, nq_v, nq_s, lst, sem):
-    off = [reg_ref[:, r, :] for r in range(3)]
-    frc = [reg_ref[:, 3 + r, :] for r in range(3)]
-    cnt = reg_ref[:, 6, :]
+    off = [reg_ref[:, 4 + r, :] for r in range(3)]
+    frc = [reg_ref[:, r, :] for r in range(3)]
+    cnt = reg_ref[:, 3, :]
     nq = jnp.where(cnt > 32.0, 1, 0) + jnp.where(cnt > 64.0, 1, 0) + jnp.where(cnt > 96.0, 1, 0) + 1
     nq_v[...] = nq.astype(jnp.int32)
     cp = pltpu.make_async_copy(nq_v, nq_s, sem)
@@ -109,9 +109,9 @@
         ko = o % 2
         ob = (xo + 1) * 16 + (yo + 1) * 4 + ko
         T = reg_ref[ob]
-        x = T[0:1] + (xo - 1).astype(F32)
-        y = T[1:2] + (yo - 1).astype(F32)
-        z = T[2:3] + (ko - 1).astype(F32)
+        x = T[4:5] + (xo - 1).astype(F32)
+        y = T[5:6] + (yo - 1).astype(F32)
+        z = T[6:7] + (ko - 1).astype(F32)
         tp = [x, y, z]
         m3 = split3(x * x + y * y + z * z + 0.01)
         o1 = jnp.ones((1, 128), F32)
@@ -170,7 +170,7 @@
             ad = ad + jnp.dot(q_ref[b, 16:64], cd[j], preferred_element_type=F32)
         cv = (ac[6:9] + ac[3:6]) + ac[0:3]
         dq = (ad[32:48] + ad[16:32]) + ad[0:16]
-        live = (lax.broadcasted_iota(jnp.int32, (1, 128), 1).astype(F32) < T[6:7]).astype(F32) * NORM
+        live = (lax.broadcasted_iota(jnp.int32, (1, 128), 1).astype(F32) < T[3:4]).astype(F32) * NORM
         xf = (x * dq[0:1] + y * dq[1:2] + z * dq[2:3]) - dq[3:4]
         for a in range(3):
             v = cv[a:a + 1] + tp[a] * xf
@@ -201,27 +201,78 @@
     )(region)
 
 
-def halo(array, axis, dim):
-    n = lax.axis_size(axis)
-    up = [(i, (i + 1) % n) for i in range(n)]
-    down = [(j, i) for i, j in up]
-    last = lax.slice_in_dim(array, 1, 2, axis=dim)
-    first = lax.slice_in_dim(array, 0, 1, axis=dim)
-    before = lax.ppermute(last, axis, up)
-    after = lax.ppermute(first, axis, down)
-    return jnp.concatenate([before, array, after], axis=dim)
+def halo_kernel(off_ref, frc_ref, cnt_ref, reg_ref, send_ref, send_sems, recv_sems):
+    ix = lax.axis_index("gx")
+    iy = lax.axis_index("gy")
+    ih = lax.axis_index("ha")
+    nx = lax.axis_size("gx")
+    ny = lax.axis_size("gy")
+    peers = []
+    for dh in (1, 0):
+        for dx in (0, 1, -1):
+            for dy in (0, 1, -1):
+                if dx or dy or dh:
+                    peers.append((dx, dy, dh))
+
+    def at(p):
+        return (lax.rem(ix + p[0] + nx, nx), lax.rem(iy + p[1] + ny, ny), lax.rem(ih + p[2], 2))
+
+    barrier = pltpu.get_barrier_semaphore()
+    for p in peers:
+        pl.semaphore_signal(barrier, inc=1, device_id=at(p), device_id_type=pl.DeviceIdType.MESH)
+    lane = lax.broadcasted_iota(jnp.int32, (1, 128), 1)
+    for b in range(8):
+        n = cnt_ref[b]
+        live = (lane < n).astype(F32)
+        rows = [frc_ref[r, b:b + 1] * live for r in range(3)] + [jnp.full((1, 128), n, jnp.int32).astype(F32)]
+        rows += [off_ref[r, b:b + 1] for r in range(3)] + [jnp.zeros((1, 128), F32)]
+        tile = jnp.concatenate(rows, axis=0)
+        send_ref[b // 4, (b // 2) % 2, b % 2] = tile
+        reg_ref[1 + b // 4, 1 + (b // 2) % 2, b % 2] = tile
+    pl.semaphore_wait(barrier, len(peers))
+    span = {0: (0, 2), 1: (1, 1), -1: (0, 1)}
+    dest = {0: 1, 1: 0, -1: 3}
+    copies = []
+    for i, p in enumerate(peers):
+        (sx, lx), (sy, ly) = span[p[0]], span[p[1]]
+        copy = pltpu.make_async_remote_copy(
+            src_ref=send_ref.at[pl.ds(sx, lx), pl.ds(sy, ly)],
+            dst_ref=reg_ref.at[pl.ds(dest[p[0]], lx), pl.ds(dest[p[1]], ly), pl.ds(2 * p[2], 2)],
+            send_sem=send_sems.at[i],
+            recv_sem=recv_sems.at[i],
+            device_id=at(p),
+            device_id_type=pl.DeviceIdType.MESH,
+        )
+        copy.start()
+        copies.append(copy)
+    for copy in copies:
+        copy.wait_recv()
+    for copy in copies:
+        copy.wait_send()
+
+
+def halo_call(offsets, forces, counts):
+    return pl.pallas_call(
+        halo_kernel,
+        out_shape=jax.ShapeDtypeStruct((4, 4, 4, 8, 128), F32),
+        in_specs=[
+            pl.BlockSpec(memory_space=pltpu.VMEM),
+            pl.BlockSpec(memory_space=pltpu.VMEM),
+            pl.BlockSpec(memory_space=pltpu.SMEM),
+        ],
+        out_specs=pl.BlockSpec(memory_space=pltpu.VMEM),
+        scratch_shapes=[
+            pltpu.VMEM((2, 2, 2, 8, 128), F32),
+            pltpu.SemaphoreType.DMA((17,)),
+            pltpu.SemaphoreType.DMA((17,)),
+        ],
+        compiler_params=pltpu.CompilerParams(collective_id=0, has_side_effects=True),
+    )(offsets, forces, counts)
 
 
 def on_device(offsets, forces, counts):
-    slots = jnp.arange(128, dtype=jnp.int32)
-    live = (slots < counts[..., None]).astype(F32)
-    rows = jnp.concatenate([offsets, forces * live[None]], axis=0).transpose(1, 2, 3, 0, 4)
-    cnt = jnp.broadcast_to(counts.astype(F32)[..., None, None], (2, 2, 2, 2, 128))
-    packed = jnp.concatenate([rows, cnt], axis=3)
-    ext = halo(halo(packed, "gx", 0), "gy", 1)
-    other = lax.ppermute(ext, "ha", [(0, 1), (1, 0)])
-    region = jnp.concatenate([ext, other], axis=2).reshape(64, 8, 128)
-    return near_call(region).reshape(3, 2, 2, 2, 128)
+    region = halo_call(offsets.reshape(3, 8, 128), forces.reshape(3, 8, 128), counts.reshape(8))
+    return near_call(region.reshape(64, 8, 128)).reshape(3, 2, 2, 2, 128)
 
 
 def solution(mesh):

time: 82 us -> 69 us (0.84)
  Pallas kernels: 35.4 us -> 67.1 us
  starting transfers between devices: 31 us -> 0 us
  waiting for transfers between devices: 12.5 us -> 0 us
  other arithmetic: 1.79 us -> 0 us
    pallas_call x0 -> x1, Pallas kernels: none -> 33.6 us  [halo_call(): pl.pallas_call(halo_kernel, out_shape=jax.ShapeDtypeStruct((4, 4, 4, 8, 1...]
    ppermute x5 -> x0, starting transfers between devices: 31 us -> none  [the longest x2 17.4 us: halo(): after = lax.ppermute(first, axis, down)]
    ppermute x5 -> x0, waiting for transfers between devices: 12.5 us -> none  [the longest x1 8.35 us: on_device(): other = lax.ppermute(ext, 'ha', [(0, 1), (1, 0)])]
    pallas_call x1, Pallas kernels: 35.4 us -> 33.6 us  [near_call(): pl.pallas_call(near_kernel, out_shape=jax.ShapeDtypeStruct((3, 8, 128), F...]
    concatenate x1 -> x0, local copies, waits for them, and re-layouts: 0.85 us -> none  [on_device(): region = jnp.concatenate([ext, other], axis=2).reshape(64, 8, 128)]
    convert_element_type x2 -> x0, other arithmetic: 0.83 us -> none  [the longest x1 0.76 us: on_device(): counts.astype(F32)[..., None, None]]
  transfers between devices with their start and end apart: 5 -> 0, of which waited for: 4 -> 0; matrix products, arithmetic and copies ran while one was open for 0% -> 0% of each run, Pallas kernels for 0% -> 0%
where the time goes in v2:
time: 69 us; the launch traced here: 68.4 us
  Pallas kernels  67.1 us (97%)
  local copies, waits for them, and re-layouts  1.27 us (2%)
    pallas_call x1, Pallas kernels, halo_call(): pl.pallas_call(halo_kernel, out_shape=jax.ShapeDtypeStruct((4, 4, 4, 8, 1...  33.6 us
    pallas_call x1, Pallas kernels, near_call(): pl.pallas_call(near_kernel, out_shape=jax.ShapeDtypeStruct((3, 8, 128), F...  33.6 us

profile of v2, /device:TPU:1, one launch (start us, length us, event | category | flops | bytes accessed | tf_op | source)
XLA Modules:
  0.0 68.4 jit_solution(3194355757805475339)
XLA Ops:
  0.0 0.0 copy-start
  0.0 0.7 copy-done
  0.7 0.6 reshape.17.cnt_ref
  1.3 33.6 %shard_map.37 = f32[4,4,4,8,128]{4,3,2,1,0:T(8,128)} custom-call(f32[3,8,128]{2,1,0:T(8,128)} %bitcast.5, f32[3,8,128]{2,1,0:T(8,128)} %bitcast.6, s32[8]{0:T(128)} %reshape.17.cnt_ref), custom_call_target="tpu_custom_call" | custom-call | tf_op jit(solution)/shard_map/pallas_call | solution.py:255
  34.9 33.6 %shard_map.38 = f32[3,8,128]{2,1,0:T(8,128)} custom-call(f32[64,8,128]{2,1,0:T(8,128)} %bitcast.4), custom_call_target="tpu_custom_call" | custom-call | tf_op jit(solution)/shard_map/pallas_call | solution.py:183
Async XLA Ops:
  0.0 0.7 copy-start

commit v3 on v2

v3 whole, which is shorter than its diff:
```python
import math

import jax
import jax.numpy as jnp
from jax import lax
from jax.experimental import pallas as pl
from jax.experimental.pallas import tpu as pltpu
from jax.sharding import PartitionSpec as P


GAUSS = 4.0 / math.sqrt(math.pi)
NORM = 1.0 / (8.0 * math.pi)
ERFCX = (-6.605853591129529e-05, 0.2835500330769051, 0.2685154202156198, 0.31675806246707194,
         -0.03963002369445217, 0.48597127806071433, -0.4204782835714706, 0.1053890269858883)
BATCH = 16
NJ = 7
TAIL = 22
F32 = jnp.float32
BF16 = jnp.bfloat16


def split3(v):
    a = v.astype(BF16).astype(F32)
    r = v - a
    b = r.astype(BF16).astype(F32)
    return a, b, r - b


def coefs(sq, keep=None):
    rs = lax.rsqrt(sq)
    rad = sq * rs
    z = rad + 1.0
    t = lax.rsqrt(z * z)
    p = ERFCX[7]
    for q in ERFCX[6::-1]:
        p = p * t + q
    e = rs * p
    g = jnp.exp2((-4.0 * math.log2(math.e)) * sq)
    if keep is not None:
        g = jnp.where(keep, g, 0.0)
    a = (8.0 * GAUSS) * sq - 3.0 * GAUSS
    c = g * (e + a)
    d = (g * (rs * rs)) * ((e - a) - 2.0 * GAUSS)
    ch = c.astype(BF16)
    cl = (c - ch.astype(F32)).astype(BF16)
    dh = d.astype(BF16)
    dl = (d - dh.astype(F32)).astype(BF16)
    return ch, cl, dh, dl


def flt(v):
    return float(v) if isinstance(v, int) else v.astype(F32)


def bin_of(o, j):
    return ((o >> 2) + j // 9) * 16 + (((o >> 1) & 1) + (j // 3) % 3) * 4 + (((o & 1) + j % 3 + 3) & 3)


def near_kernel(reg_ref, out_ref, a_ref, q_ref, cc, cd, sqb, acc_c, acc_d, nq_s, lst, tab, cnts):
    sub = lax.broadcasted_iota(jnp.int32, (8, 128), 0)

    def shift_of(b):
        zi = b & 3
        sx = ((b >> 4) - 2).astype(F32)
        sy = (((b >> 2) & 3) - 2).astype(F32)
        sz = jnp.where(zi == 3, -2, zi - 1).astype(F32)
        return sx, sy, sz

    def prep(b):
        tile = reg_ref[b]
        sx, sy, sz = shift_of(b)
        c = tile[3, 0]
        nq_s[b] = (1 + jnp.where(c > 32.0, 1, 0) + jnp.where(c > 64.0, 1, 0) + jnp.where(c > 96.0, 1, 0)).astype(jnp.int32)
        f = tile[0:3]
        x = tile[4:5] + sx
        y = tile[5:6] + sy
        z = tile[6:7] + sz
        n = x * x + y * y + z * z
        m2 = jnp.concatenate([-2.0 * x, -2.0 * y, -2.0 * z, n], axis=0)
        r1, r2, r3 = split3(m2)
        feat = jnp.concatenate([r1, r1, r1, r2, r2, r3, jnp.ones((8, 128), F32)], axis=0)
        at = feat.astype(BF16).astype(F32).T.astype(BF16)
        for u in range(4):
            a_ref[4 * b + u] = at[32 * u:32 * (u + 1)]
        w = x * f[0:1] + y * f[1:2] + z * f[2:3]
        g4 = jnp.concatenate([f, w], axis=0)
        p1 = jnp.concatenate([g4, x * g4], axis=0)
        p2 = jnp.concatenate([y * g4, z * g4], axis=0)
        a3 = split3(p1)
        b3 = split3(p2)
        q = jnp.concatenate([a3[0], a3[1], a3[0], b3[0], a3[1], b3[1], a3[2], b3[2]], axis=0)
        q_ref[b] = q.astype(BF16)

    @pl.loop(0, 16)
    def _(i):
        for k in range(4):
            prep(4 * i + k)

    q_ref[64] = jnp.zeros((64, 128), BF16)
    for i in range(60):
        tab[i] = 64
    rowi = lax.broadcasted_iota(jnp.int32, (128, 128), 0)
    lani = lax.broadcasted_iota(jnp.int32, (128, 128), 1)

    def target(o):
        tile = reg_ref[bin_of(o, 13)]
        x = tile[4:5] + flt((o >> 2) - 1)
        y = tile[5:6] + flt(((o >> 1) & 1) - 1)
        z = tile[6:7] + flt((o & 1) - 1)
        return tile, x, y, z

    def reduce_bins(o1, base, js):
        ac = acc_c[...]
        ad = acc_d[...]
        for j in js:
            q = q_ref[tab[o1 * 64 + j]]
            q2 = jnp.concatenate([q, q], axis=1)
            k = base + 8 * j if isinstance(j, int) else base + 8 * jnp.minimum(j, 26)
            ac = ac + jnp.dot(q2[0:16], cc[pl.ds(k, 8)].reshape(256, 128), preferred_element_type=F32)
            ad = ad + jnp.dot(q2[16:64], cd[pl.ds(k, 8)].reshape(256, 128), preferred_element_type=F32)
        acc_c[...] = ac
        acc_d[...] = ad

    def finish(o):
        tile, x, y, z = target(o)
        tp = [x, y, z]
        cv = acc_c[8:11] + acc_c[0:3]
        dq = (acc_d[32:48] + acc_d[16:32]) + acc_d[0:16]
        live = (lax.broadcasted_iota(jnp.int32, (1, 128), 1).astype(F32) < tile[3:4]).astype(F32) * NORM
        xf = (x * dq[0:1] + y * dq[1:2] + z * dq[2:3]) - dq[3:4]
        for a in range(3):
            i = 4 + 4 * a
            v = cv[a:a + 1] + tp[a] * xf
            v = v - ((x * dq[i:i + 1] + y * dq[i + 1:i + 2] + z * dq[i + 2:i + 3]) - dq[i + 3:i + 4])
            out_ref[a, pl.ds(o, 1)] = v * live

    acc_c[...] = jnp.zeros_like(acc_c)
    acc_d[...] = jnp.zeros_like(acc_d)

    def build(o):
        start = (o & 1) * 160
        n = start
        row = (o + 1) * 64
        corner = (o >> 2) * 16 + ((o >> 1) & 1) * 4
        zs = [((o & 1) + k + 3) & 3 for k in range(3)]
        zb = [corner + z for z in zs]
        for j in range(27):
            b = zb[j % 3] + ((j // 9) * 16 + (j // 3 % 3) * 4)
            tab[row + j] = b
            if j == 13:
                continue
            e = (zb[j % 3] << 10) + (((j // 9) * 16 + (j // 3 % 3) * 4) * 1024 + j * 8)
            for u in range(4):
                lst[n + u] = e + u * 257
            n = n + nq_s[b]
        for j in range(27, 27 + TAIL):
            tab[row + j] = 64
        for u in range(2 * BATCH):
            lst[n + u] = zb[0] << 10
        cnts[o] = n - start

    build(0)

    @pl.loop(0, 8)
    def _(o):
        here = (o & 1) * 216

        @pl.when(o < 2)
        def _():
            blank = jnp.zeros((96, 128), F32).astype(BF16).reshape(3, 32, 128)
            for j in range(27):
                for w in (1, 5):
                    cc[pl.ds(here + 8 * j + w, 3)] = blank
                    cd[pl.ds(here + 8 * j + w, 3)] = blank

        there = 216 - here
        tile, x, y, z = target(o)
        t1, t2, t3 = split3(jnp.concatenate([x, y, z], axis=0))
        m1, m2, m3 = split3(x * x + y * y + z * z + 0.01)
        one = jnp.ones((1, 128), F32)
        zero = jnp.zeros((1, 128), F32)
        bmat = jnp.concatenate(
            [t1, one, t2, zero, t3, zero, t1, one, t2, zero, t1, one, m1, m2, m3, zero, zero, zero, zero, zero], axis=0
        ).astype(BF16)
        n = cnts[o]
        first = (o & 1) * 160
        ob = bin_of(o, 13)
        aown = a_ref[pl.ds(4 * ob, 4)].reshape(128, 32)
        sq = jnp.dot(aown, bmat, preferred_element_type=F32)

        def distances(it):
            am = jnp.concatenate([a_ref[lst[first + it * BATCH + u] >> 8] for u in range(BATCH)], axis=0)
            sqb[it & 1] = jnp.dot(am, bmat, preferred_element_type=F32)

        distances(0)
        pieces = coefs(sq, rowi != lani)
        for u in range(4):
            for k in range(4):
                (cc, cd)[k // 2][here + 104 + u + 4 * (k % 2)] = pieces[k][32 * u:32 * (u + 1)]
        nit = lax.div(n + BATCH - 1, BATCH)
        build(jnp.minimum(o + 1, 7))

        @pl.loop(0, jnp.maximum(nit, -(-27 // NJ)))
        def _(it):
            it2 = jnp.minimum(it, nit - 1)
            pieces = coefs(sqb[it2 & 1])
            reduce_bins(o, there, [it * NJ + i for i in range(NJ)])
            distances(it2 + 1)
            for u in range(BATCH):
                e = here + (lst[first + it2 * BATCH + u] & 255)
                for k in range(4):
                    (cc, cd)[k // 2][e + 4 * (k % 2)] = pieces[k][32 * u:32 * (u + 1)]

        @pl.when(o > 0)
        def _():
            finish(o - 1)
        acc_c[...] = jnp.zeros_like(acc_c)
        acc_d[...] = jnp.zeros_like(acc_d)

    reduce_bins(8, 216, list(range(27)))
    finish(7)


def near_call(region):
    return pl.pallas_call(
        near_kernel,
        out_shape=jax.ShapeDtypeStruct((3, 8, 128), F32),
        in_specs=[pl.BlockSpec(memory_space=pltpu.VMEM)],
        out_specs=pl.BlockSpec(memory_space=pltpu.VMEM),
        scratch_shapes=[
            pltpu.VMEM((256, 32, 32), BF16),
            pltpu.VMEM((65, 64, 128), BF16),
            pltpu.VMEM((432, 32, 128), BF16),
            pltpu.VMEM((432, 32, 128), BF16),
            pltpu.VMEM((2, 32 * BATCH, 128), F32),
            pltpu.VMEM((16, 128), F32),
            pltpu.VMEM((48, 128), F32),
            pltpu.SMEM((64,), jnp.int32),
            pltpu.SMEM((320,), jnp.int32),
            pltpu.SMEM((576,), jnp.int32),
            pltpu.SMEM((8,), jnp.int32),
        ],
    )(region)


def halo_kernel(off_ref, frc_ref, cnt_ref, reg_ref, send_ref, send_sems, recv_sems):
    ix = lax.axis_index("gx")
    iy = lax.axis_index("gy")
    ih = lax.axis_index("ha")
    nx = lax.axis_size("gx")
    ny = lax.axis_size("gy")
    sides = [(dx, dy) for dx in (0, 1, -1) for dy in (0, 1, -1) if dx or dy]
    columns = [(sx, sy) for sx in range(2) for sy in range(2)]

    def at(dx, dy):
        return (lax.rem(ix + dx + nx, nx), lax.rem(iy + dy + ny, ny), ih)

    partner = (ix, iy, 1 - ih)
    barrier = pltpu.get_barrier_semaphore()
    for device in [partner] + [at(*p) for p in sides]:
        pl.semaphore_signal(barrier, inc=1, device_id=device, device_id_type=pl.DeviceIdType.MESH)
    lane = lax.broadcasted_iota(jnp.int32, (1, 128), 1)
    for b in range(8):
        n = cnt_ref[b // 4, (b // 2) % 2, b % 2]
        live = (lane < n).astype(F32)
        rows = [frc_ref[r, b:b + 1] * live for r in range(3)] + [jnp.full((1, 128), n, jnp.int32).astype(F32)]
        rows += [off_ref[r, b:b + 1] for r in range(3)] + [jnp.zeros((1, 128), F32)]
        tile = jnp.concatenate(rows, axis=0)
        send_ref[b // 4, (b // 2) % 2, b % 2] = tile
        reg_ref[1 + b // 4, 1 + (b // 2) % 2, b % 2] = tile
    pl.semaphore_wait(barrier, 9)
    copies = []

    def send(src, dst, device):
        i = len(copies)
        copy = pltpu.make_async_remote_copy(
            src_ref=src,
            dst_ref=dst,
            send_sem=send_sems.at[i],
            recv_sem=recv_sems.at[i],
            device_id=device,
            device_id_type=pl.DeviceIdType.MESH,
        )
        copy.start()
        copies.append(copy)

    for sx, sy in columns:
        send(send_ref.at[sx, sy], reg_ref.at[1 + sx, 1 + sy, pl.ds(2, 2)], partner)
    span = {0: (0, 2), 1: (1, 1), -1: (0, 1)}
    dest = {0: 1, 1: 0, -1: 3}
    for dx, dy in sides:
        (sx, lx), (sy, ly) = span[dx], span[dy]
        send(
            send_ref.at[pl.ds(sx, lx), pl.ds(sy, ly)],
            reg_ref.at[pl.ds(dest[dx], lx), pl.ds(dest[dy], ly), pl.ds(0, 2)],
            at(dx, dy),
        )
    for i, (sx, sy) in enumerate(columns):
        copies[i].wait_recv()
        dx, dy = 2 * sx - 1, 2 * sy - 1
        src = reg_ref.at[1 + sx, 1 + sy, pl.ds(2, 2)]
        for px, py in ((dx, 0), (0, dy), (dx, dy)):
            tx = dest[px] if px else 1 + sx
            ty = dest[py] if py else 1 + sy
            send(src, reg_ref.at[tx, ty, pl.ds(2, 2)], at(px, py))
    for copy in copies[4:]:
        copy.wait_recv()
    for copy in copies:
        copy.wait_send()


def halo_call(offsets, forces, counts):
    return pl.pallas_call(
        halo_kernel,
        out_shape=jax.ShapeDtypeStruct((4, 4, 4, 8, 128), F32),
        in_specs=[
            pl.BlockSpec(memory_space=pltpu.VMEM),
            pl.BlockSpec(memory_space=pltpu.VMEM),
            pl.BlockSpec(memory_space=pltpu.SMEM),
        ],
        out_specs=pl.BlockSpec(memory_space=pltpu.VMEM),
        scratch_shapes=[
            pltpu.VMEM((2, 2, 2, 8, 128), F32),
            pltpu.SemaphoreType.DMA((24,)),
            pltpu.SemaphoreType.DMA((24,)),
        ],
        compiler_params=pltpu.CompilerParams(collective_id=0, has_side_effects=True),
    )(offsets, forces, counts)


def on_device(offsets, forces, counts):
    region = halo_call(offsets.reshape(3, 8, 128), forces.reshape(3, 8, 128), counts)
    return near_call(region.reshape(64, 8, 128)).reshape(3, 2, 2, 2, 128)


def solution(mesh):
    spec = P(None, "gx", "gy", "ha", None)
    return jax.shard_map(
        on_device, mesh=mesh, in_specs=(spec, spec, P("gx", "gy", "ha")), out_specs=spec, check_vma=False
    )
```

time: 69 us -> 58.4 us (0.85)
  Pallas kernels: 67.1 us -> 57.7 us
  local copies, waits for them, and re-layouts: 1.27 us -> 0 us
    pallas_call x1, Pallas kernels: 33.6 us -> 24.9 us  [near_call(): pl.pallas_call(near_kernel, out_shape=jax.ShapeDtypeStruct((3, 8, 128), F...]
    pallas_call x1, Pallas kernels: 33.6 us -> 32.7 us  [halo_call(): pl.pallas_call(halo_kernel, out_shape=jax.ShapeDtypeStruct((4, 4, 4, 8, 1...]
where the time goes in v3:
time: 58.4 us; the launch traced here: 57.7 us
  Pallas kernels  57.7 us (99%)
    pallas_call x1, Pallas kernels, halo_call(): pl.pallas_call(halo_kernel, out_shape=jax.ShapeDtypeStruct((4, 4, 4, 8, 1...  32.7 us
    pallas_call x1, Pallas kernels, near_call(): pl.pallas_call(near_kernel, out_shape=jax.ShapeDtypeStruct((3, 8, 128), F...  24.9 us

profile of v3, /device:TPU:1, one launch (start us, length us, event | category | flops | bytes accessed | tf_op | source)
XLA Modules:
  0.0 57.7 jit_solution(5480847085891298174)
XLA Ops:
  0.0 32.7 %shard_map.37 = f32[4,4,4,8,128]{4,3,2,1,0:T(8,128)} custom-call(f32[3,8,128]{2,1,0:T(8,128)} %bitcast.5, f32[3,8,128]{2,1,0:T(8,128)} %bitcast.6, s32[2,2,2]{2,1,0:T(2,128)} %cnt_ref.1), custom_call_target="tpu_custom_call" | custom-call | tf_op jit(solution)/shard_map/pallas_call | solution.py:313
  32.7 24.9 %shard_map.38 = f32[3,8,128]{2,1,0:T(8,128)} custom-call(f32[64,8,128]{2,1,0:T(8,128)} %bitcast.4), custom_call_target="tpu_custom_call" | custom-call | tf_op jit(solution)/shard_map/pallas_call | solution.py:225

commit v4 on v3

v4 whole, which is shorter than its diff:
```python
import math

import jax
import jax.numpy as jnp
from jax import lax
from jax.experimental import pallas as pl
from jax.experimental.pallas import tpu as pltpu
from jax.sharding import PartitionSpec as P


GAUSS = 4.0 / math.sqrt(math.pi)
NORM = 1.0 / (8.0 * math.pi)
ERFCX = (-6.605853591129529e-05, 0.2835500330769051, 0.2685154202156198, 0.31675806246707194,
         -0.03963002369445217, 0.48597127806071433, -0.4204782835714706, 0.1053890269858883)
F32 = jnp.float32
BF16 = jnp.bfloat16
MESH = pl.DeviceIdType.MESH


def split3(v):
    a = v.astype(BF16).astype(F32)
    r = v - a
    b = r.astype(BF16).astype(F32)
    return a, b, r - b


def coefs(sq, keep=None):
    rs = lax.rsqrt(sq)
    z = sq * rs + 1.0
    t = lax.rsqrt(z * z)
    p = ERFCX[7]
    for q in ERFCX[6::-1]:
        p = p * t + q
    e = rs * p
    g = jnp.exp2((-4.0 * math.log2(math.e)) * sq)
    if keep is not None:
        g = jnp.where(keep, g, 0.0)
    a = (8.0 * GAUSS) * sq - 3.0 * GAUSS
    c = g * (e + a)
    d = (g * (rs * rs)) * ((e - a) - 2.0 * GAUSS)
    ch = c.astype(BF16)
    cl = (c - ch.astype(F32)).astype(BF16)
    dh = d.astype(BF16)
    dl = (d - dh.astype(F32)).astype(BF16)
    return ch, cl, dh, dl


def parts_of(o):
    return lax.div(o, 4), lax.rem(lax.div(o, 2), 2), lax.rem(o, 2)


def pair_own(p):
    o, s = lax.div(p, 8), lax.rem(p, 8)
    return 1 + lax.div(s, 4), 1 + lax.rem(lax.div(s, 2), 2), lax.rem(s, 2), o


def pair_y_near(p):
    o, s = lax.div(p, 4), lax.rem(p, 4)
    return 1 + lax.div(s, 2), 3 * parts_of(o)[1], lax.rem(s, 2), o


def pair_mid_far(p):
    o, s = lax.div(p, 4), lax.rem(p, 4)
    return 1 + lax.div(s, 2), 1 + lax.rem(s, 2), 3 - lax.rem(o, 2), o


def pair_y_far(p):
    o, s = lax.div(p, 2), lax.rem(p, 2)
    return 1 + s, 3 * parts_of(o)[1], 3 - lax.rem(o, 2), o


def pair_x_near(side):
    def pair(p):
        t, s = lax.div(p, 6), lax.rem(p, 6)
        return 3 * side, lax.div(t, 2) + lax.div(s, 2), lax.rem(s, 2), 4 * side + t
    return pair


def pair_x_far(side):
    def pair(p):
        t, s = lax.div(p, 3), lax.rem(p, 3)
        return 3 * side, lax.div(t, 2) + s, 3 - lax.rem(t, 2), 4 * side + t
    return pair


def bins_mid(y0, ystep, z0):
    def new(n):
        return 1 + lax.div(n, 4), y0 + ystep * lax.rem(lax.div(n, 2), 2), z0 + lax.rem(n, 2)
    return new


def bins_side(side, z0):
    def new(n):
        return 3 * side, lax.div(n, 2), z0 + lax.rem(n, 2)
    return new


def near_kernel(off_ref, frc_ref, cnt_ref, out_ref, reg_ref, send_ref, a_ref, q_ref, b_ref, cc, cd, sqb, acc_c, acc_d,
                send_sems, recv_sems):
    ix = lax.axis_index("gx")
    iy = lax.axis_index("gy")
    ih = lax.axis_index("ha")
    nx = lax.axis_size("gx")
    ny = lax.axis_size("gy")
    sides = [(dx, dy) for dx in (0, 1, -1) for dy in (0, 1, -1) if dx or dy]
    columns = [(sx, sy) for sx in range(2) for sy in range(2)]

    def at(dx, dy):
        return (lax.rem(ix + dx + nx, nx), lax.rem(iy + dy + ny, ny), ih)

    partner = (ix, iy, 1 - ih)
    barrier = pltpu.get_barrier_semaphore()
    for device in [partner] + [at(*p) for p in sides]:
        pl.semaphore_signal(barrier, inc=1, device_id=device, device_id_type=MESH)

    lane = lax.broadcasted_iota(jnp.int32, (1, 128), 1)
    one = jnp.ones((1, 128), F32)
    zero = jnp.zeros((1, 128), F32)
    for b in range(8):
        bx, by, bz = b // 4, (b // 2) % 2, b % 2
        n = cnt_ref[bx, by, bz]
        live = (lane < n).astype(F32)
        rows = [frc_ref[r, b:b + 1] * live for r in range(3)] + [live]
        rows += [off_ref[r, b:b + 1] for r in range(3)] + [zero]
        tile = jnp.concatenate(rows, axis=0)
        send_ref[bx, by, bz] = tile
        reg_ref[1 + bx, 1 + by, bz] = tile
        x = tile[4:5] + float(bx - 1)
        y = tile[5:6] + float(by - 1)
        z = tile[6:7] + float(bz - 1)
        t1, t2, t3 = split3(jnp.concatenate([x, y, z], axis=0))
        m1, m2, m3 = split3(x * x + y * y + z * z + 0.01)
        b_ref[b] = jnp.concatenate(
            [t1, one, t2, zero, t3, zero, t1, one, t2, zero, t1, one, m1, m2, m3, zero, zero, zero, zero, zero], axis=0
        ).astype(BF16)
    acc_c[...] = jnp.zeros_like(acc_c)
    acc_d[...] = jnp.zeros_like(acc_d)
    cc[...] = jnp.zeros((4, 256, 128), F32).astype(BF16)
    cd[...] = jnp.zeros((4, 256, 128), F32).astype(BF16)
    sub = lax.broadcasted_iota(jnp.int32, (128, 128), 0)
    diff = lax.broadcasted_iota(jnp.int32, (128, 128), 1) - sub

    def prep(new):
        @pl.loop(0, 2)
        def _(i):
            for k in range(4):
                X, Y, Z = new(4 * i + k)
                b = X * 16 + Y * 4 + Z
                tile = reg_ref[X, Y, Z]
                f = tile[0:3]
                x = tile[4:5] + jnp.asarray(X - 2).astype(F32)
                y = tile[5:6] + jnp.asarray(Y - 2).astype(F32)
                z = tile[6:7] + jnp.asarray(Z - 1 - 4 * lax.div(Z, 3)).astype(F32)
                n = x * x + y * y + z * z
                r1, r2, r3 = split3(jnp.concatenate([-2.0 * x, -2.0 * y, -2.0 * z, n], axis=0))
                feat = jnp.concatenate([r1, r1, r1, r2, r2, r3, jnp.ones((8, 128), F32)], axis=0)
                a_ref[b] = feat.T.astype(BF16)
                w = x * f[0:1] + y * f[1:2] + z * f[2:3]
                g4 = jnp.concatenate([f, w], axis=0)
                a3 = split3(jnp.concatenate([g4, x * g4], axis=0))
                b3 = split3(jnp.concatenate([y * g4, z * g4], axis=0))
                q = jnp.concatenate([a3[0], a3[1], a3[0], b3[0], a3[1], b3[1], a3[2], b3[2]], axis=0)
                q_ref[b] = q.astype(BF16)

    def reduce_pairs(pairs):
        for k, (b, o) in enumerate(pairs):
            q = q_ref[b]
            q2 = jnp.concatenate([q, q], axis=1)
            acc_c[o] = acc_c[o] + jnp.dot(q2[0:16], cc[k], preferred_element_type=F32)
            acc_d[o] = acc_d[o] + jnp.dot(q2[16:64], cd[k], preferred_element_type=F32)

    def distances(pairs):
        for k, (b, o) in enumerate(pairs):
            sqb[k] = jnp.dot(a_ref[b], b_ref[o], preferred_element_type=F32)

    def flat(pair, i):
        out = []
        for k in range(4):
            X, Y, Z, o = pair(jnp.asarray(4 * i + k, jnp.int32))
            out.append((X * 16 + Y * 4 + Z, o))
        return out

    def phase(pair, lo, hi, last, mask=False):
        distances(flat(pair, lo))
        n = hi - lo

        @pl.loop(0, n)
        def _(i):
            began = lax.div(i + n - 1, n)
            now = flat(pair, lo + i - began)
            pending = [(b * began + pb * (1 - began), o * began + po * (1 - began)) for (b, o), (pb, po) in zip(now, last)]
            reduce_pairs(pending)
            for k in range(4):
                keep = None
                if mask:
                    p = 4 * (lo + i) + k
                    same = lax.rem(lax.div(p, 8) - lax.rem(p, 8) + 8, 8)
                    keep = diff != same * 1000
                ch, cl, dh, dl = coefs(sqb[k], keep)
                cc[k, 0:128] = ch
                cc[k, 128:256] = cl
                cd[k, 0:128] = dh
                cd[k, 128:256] = dl
            distances(flat(pair, lo + i + 1 - lax.div(i + 1, n)))

        return [tuple(v) for v in flat(pair, hi - 1)]

    copies = []

    def send(src, dst, device):
        i = len(copies)
        copy = pltpu.make_async_remote_copy(
            src_ref=src, dst_ref=dst, send_sem=send_sems.at[i], recv_sem=recv_sems.at[i],
            device_id=device, device_id_type=MESH,
        )
        copy.start()
        copies.append(copy)

    span = {0: (0, 2), 1: (1, 1), -1: (0, 1)}
    dest = {0: 1, 1: 0, -1: 3}

    prep(bins_mid(1, 1, 0))
    last = flat(pair_own, 0)
    last = phase(pair_own, 0, SPLIT, last, mask=True)

    pl.semaphore_wait(barrier, 9)
    for sx, sy in columns:
        send(send_ref.at[sx, sy], reg_ref.at[1 + sx, 1 + sy, pl.ds(2, 2)], partner)
    for dx, dy in sides:
        (sx, lx), (sy, ly) = span[dx], span[dy]
        send(
            send_ref.at[pl.ds(sx, lx), pl.ds(sy, ly)],
            reg_ref.at[pl.ds(dest[dx], lx), pl.ds(dest[dy], ly), pl.ds(0, 2)],
            at(dx, dy),
        )
    near = {p: 4 + i for i, p in enumerate(sides)}
    if SPLIT < 16:
        last = phase(pair_own, SPLIT, 16, last, mask=True)

    def arrive(which):
        for i in which:
            copies[i].wait_recv()

    arrive([near[0, 1], near[0, -1]])
    prep(bins_mid(0, 3, 0))
    last = phase(pair_y_near, 0, 8, last)
    far = {}
    for i, (sx, sy) in enumerate(columns):
        copies[i].wait_recv()
        dx, dy = 2 * sx - 1, 2 * sy - 1
        src = reg_ref.at[1 + sx, 1 + sy, pl.ds(2, 2)]
        for px, py in ((dx, 0), (0, dy), (dx, dy)):
            tx = dest[px] if px else 1 + sx
            ty = dest[py] if py else 1 + sy
            far.setdefault(px, []).append(len(copies))
            send(src, reg_ref.at[tx, ty, pl.ds(2, 2)], at(px, py))
    prep(bins_mid(1, 1, 2))
    last = phase(pair_mid_far, 0, 8, last)
    arrive([near[-1, dy] for dy in (0, 1, -1)])
    prep(bins_side(1, 0))
    last = phase(pair_x_near(1), 0, 6, last)
    arrive(far[0])
    prep(bins_mid(0, 3, 2))
    last = phase(pair_y_far, 0, 4, last)
    arrive(far[-1])
    prep(bins_side(1, 2))
    last = phase(pair_x_far(1), 0, 3, last)
    arrive([near[1, dy] for dy in (0, 1, -1)])
    prep(bins_side(0, 0))
    last = phase(pair_x_near(0), 0, 6, last)
    arrive(far[1])
    prep(bins_side(0, 2))
    last = phase(pair_x_far(0), 0, 3, last)
    reduce_pairs(last)

    for o in range(8):
        tile = reg_ref[1 + o // 4, 1 + (o // 2) % 2, o % 2]
        x = tile[4:5] + float(o // 4 - 1)
        y = tile[5:6] + float((o // 2) % 2 - 1)
        z = tile[6:7] + float(o % 2 - 1)
        tp = [x, y, z]
        cv = acc_c[o, 8:11] + acc_c[o, 0:3]
        dq = (acc_d[o, 32:48] + acc_d[o, 16:32]) + acc_d[o, 0:16]
        live = tile[3:4] * NORM
        xf = (x * dq[0:1] + y * dq[1:2] + z * dq[2:3]) - dq[3:4]
        for a in range(3):
            i = 4 + 4 * a
            v = cv[a:a + 1] + tp[a] * xf
            v = v - ((x * dq[i:i + 1] + y * dq[i + 1:i + 2] + z * dq[i + 2:i + 3]) - dq[i + 3:i + 4])
            out_ref[a, o:o + 1] = v * live
    for copy in copies:
        copy.wait_send()


SPLIT = 16


def on_device(offsets, forces, counts):
    vel = pl.pallas_call(
        near_kernel,
        out_shape=jax.ShapeDtypeStruct((3, 8, 128), F32),
        in_specs=[
            pl.BlockSpec(memory_space=pltpu.VMEM),
            pl.BlockSpec(memory_space=pltpu.VMEM),
            pl.BlockSpec(memory_space=pltpu.SMEM),
        ],
        out_specs=pl.BlockSpec(memory_space=pltpu.VMEM),
        scratch_shapes=[
            pltpu.VMEM((4, 4, 4, 8, 128), F32),
            pltpu.VMEM((2, 2, 2, 8, 128), F32),
            pltpu.VMEM((64, 128, 32), BF16),
            pltpu.VMEM((64, 64, 128), BF16),
            pltpu.VMEM((8, 32, 128), BF16),
            pltpu.VMEM((4, 256, 128), BF16),
            pltpu.VMEM((4, 256, 128), BF16),
            pltpu.VMEM((4, 128, 128), F32),
            pltpu.VMEM((8, 16, 128), F32),
            pltpu.VMEM((8, 48, 128), F32),
            pltpu.SemaphoreType.DMA((24,)),
            pltpu.SemaphoreType.DMA((24,)),
        ],
        compiler_params=pltpu.CompilerParams(collective_id=0, has_side_effects=True),
    )(offsets.reshape(3, 8, 128), forces.reshape(3, 8, 128), counts)
    return vel.reshape(3, 2, 2, 2, 128)


def solution(mesh):
    spec = P(None, "gx", "gy", "ha", None)
    return jax.shard_map(
        on_device, mesh=mesh, in_specs=(spec, spec, P("gx", "gy", "ha")), out_specs=spec, check_vma=False
    )
```

time: 58.4 us -> 49.2 us (0.84)
  Pallas kernels: 57.7 us -> 47.4 us
  local copies, waits for them, and re-layouts: 0 us -> 1.31 us
    pallas_call x2 -> x1, Pallas kernels: 57.7 us -> 47.4 us  [on_device(): pl.pallas_call(near_kernel, out_shape=jax.ShapeDtypeStruct((3, 8, 128), F...]
    unnamed x0 -> x1, local copies, waits for them, and re-layouts: none -> 1.31 us
where the time goes in v4:
time: 49.2 us; the launch traced here: 48.8 us
  Pallas kernels  47.4 us (96%)
  local copies, waits for them, and re-layouts  1.31 us (3%)
    pallas_call x1, Pallas kernels, on_device(): pl.pallas_call(near_kernel, out_shape=jax.ShapeDtypeStruct((3, 8, 128), F...  47.4 us
    unnamed x1, local copies, waits for them, and re-layouts  1.31 us

profile of v4, /device:TPU:1, one launch (start us, length us, event | category | flops | bytes accessed | tf_op | source)
XLA Modules:
  0.0 48.8 jit_solution(10551287783169309634)
XLA Ops:
  0.0 47.4 %shard_map.37 = f32[3,8,128]{2,1,0:T(8,128)} custom-call(f32[3,8,128]{2,1,0:T(8,128)} %bitcast.4, f32[3,8,128]{2,1,0:T(8,128)} %bitcast.5, s32[2,2,2]{2,1,0:T(2,128)} %cnt_ref.1), custom_call_target="tpu_custom_call" | custom-call | tf_op jit(solution)/shard_map/pallas_call | solution.py:299
  47.4 1.3 %copy.5 = f32[3,2,2,2,128]{4,3,2,1,0:T(2,128)} copy(f32[3,2,2,2,128]{4,3,2,1,0:T(2,128)} %bitcast.3) | data formatting | bytes 24576

commit v5 on v4

--- a/solution.py
+++ b/solution.py
@@ -15,6 +15,7 @@
 F32 = jnp.float32
 BF16 = jnp.bfloat16
 MESH = pl.DeviceIdType.MESH
+FORMS = ((1.0, 0.0), (8.0 * GAUSS, -3.0 * GAUSS), (8.0 * GAUSS, -GAUSS), (-4.0 * math.log2(math.e), 0.0))
 
 
 def split3(v):
@@ -24,7 +25,7 @@
     return a, b, r - b
 
 
-def coefs(sq, keep=None):
+def coefs(sq, ac, ad, arg, keep=None):
     rs = lax.rsqrt(sq)
     z = sq * rs + 1.0
     t = lax.rsqrt(z * z)
@@ -32,12 +33,11 @@
     for q in ERFCX[6::-1]:
         p = p * t + q
     e = rs * p
-    g = jnp.exp2((-4.0 * math.log2(math.e)) * sq)
+    g = jnp.exp2(arg)
     if keep is not None:
         g = jnp.where(keep, g, 0.0)
-    a = (8.0 * GAUSS) * sq - 3.0 * GAUSS
-    c = g * (e + a)
-    d = (g * (rs * rs)) * ((e - a) - 2.0 * GAUSS)
+    c = g * (e + ac)
+    d = (g * (rs * rs)) * (e - ad)
     ch = c.astype(BF16)
     cl = (c - ch.astype(F32)).astype(BF16)
     dh = d.astype(BF16)
@@ -45,41 +45,36 @@
     return ch, cl, dh, dl
 
 
-def parts_of(o):
-    return lax.div(o, 4), lax.rem(lax.div(o, 2), 2), lax.rem(o, 2)
-
-
-def pair_own(p):
-    o, s = lax.div(p, 8), lax.rem(p, 8)
-    return 1 + lax.div(s, 4), 1 + lax.rem(lax.div(s, 2), 2), lax.rem(s, 2), o
-
-
-def pair_y_near(p):
-    o, s = lax.div(p, 4), lax.rem(p, 4)
-    return 1 + lax.div(s, 2), 3 * parts_of(o)[1], lax.rem(s, 2), o
-
-
-def pair_mid_far(p):
-    o, s = lax.div(p, 4), lax.rem(p, 4)
-    return 1 + lax.div(s, 2), 1 + lax.rem(s, 2), 3 - lax.rem(o, 2), o
-
-
-def pair_y_far(p):
-    o, s = lax.div(p, 2), lax.rem(p, 2)
-    return 1 + s, 3 * parts_of(o)[1], 3 - lax.rem(o, 2), o
+def odd(i):
+    return i - 2 * lax.shift_right_logical(i, 1)
+
+
+def pair_own(i, k):
+    return 16 + 16 * odd(i) + (1 + k // 2) * 4 + k % 2, lax.shift_right_logical(i, 1)
+
+
+def pair_y_near(i, k):
+    return (1 + k // 2) * 16 + 12 * odd(lax.shift_right_logical(i, 1)) + k % 2, i
+
+
+def pair_mid_far(i, k):
+    return (1 + k // 2) * 16 + (1 + k % 2) * 4 + 3 - odd(i), i
+
+
+def pair_y_far(i, k):
+    return (1 + k % 2) * 16 + 12 * odd(i) + 3 - k // 2, 2 * i + k // 2
 
 
 def pair_x_near(side):
-    def pair(p):
-        t, s = lax.div(p, 6), lax.rem(p, 6)
-        return 3 * side, lax.div(t, 2) + lax.div(s, 2), lax.rem(s, 2), 4 * side + t
+    def pair(i, k):
+        y = lax.shift_right_logical(11 * i, 5)
+        return 48 * side + (i - 2 * y) * 4 + k % 2, 4 * side + 2 * y + k // 2
     return pair
 
 
 def pair_x_far(side):
-    def pair(p):
-        t, s = lax.div(p, 3), lax.rem(p, 3)
-        return 3 * side, lax.div(t, 2) + s, 3 - lax.rem(t, 2), 4 * side + t
+    def pair(i, k):
+        return 48 * side + (k // 2 + i) * 4 + 3 - k % 2, jnp.int32(0) + 4 * side + k
     return pair
 
 
@@ -128,11 +123,13 @@
         x = tile[4:5] + float(bx - 1)
         y = tile[5:6] + float(by - 1)
         z = tile[6:7] + float(bz - 1)
-        t1, t2, t3 = split3(jnp.concatenate([x, y, z], axis=0))
-        m1, m2, m3 = split3(x * x + y * y + z * z + 0.01)
-        b_ref[b] = jnp.concatenate(
-            [t1, one, t2, zero, t3, zero, t1, one, t2, zero, t1, one, m1, m2, m3, zero, zero, zero, zero, zero], axis=0
-        ).astype(BF16)
+        m = x * x + y * y + z * z + 0.01
+        for k, (scale, extra) in enumerate(FORMS):
+            t1, t2, t3 = split3(scale * jnp.concatenate([x, y, z, one], axis=0))
+            m1, m2, m3 = split3(scale * m + extra)
+            b_ref[b, :, 128 * k:128 * (k + 1)] = jnp.concatenate(
+                [t1, t2, t3, t1, t2, t1, m1, m2, m3, zero, zero, zero, zero, zero], axis=0
+            ).astype(BF16)
     acc_c[...] = jnp.zeros_like(acc_c)
     acc_d[...] = jnp.zeros_like(acc_d)
     cc[...] = jnp.zeros((4, 256, 128), F32).astype(BF16)
@@ -162,48 +159,44 @@
                 q = jnp.concatenate([a3[0], a3[1], a3[0], b3[0], a3[1], b3[1], a3[2], b3[2]], axis=0)
                 q_ref[b] = q.astype(BF16)
 
-    def reduce_pairs(pairs):
-        for k, (b, o) in enumerate(pairs):
+    def reduce_pairs(pairs, first=0):
+        for k, (b, o) in enumerate(pairs, first):
             q = q_ref[b]
             q2 = jnp.concatenate([q, q], axis=1)
             acc_c[o] = acc_c[o] + jnp.dot(q2[0:16], cc[k], preferred_element_type=F32)
             acc_d[o] = acc_d[o] + jnp.dot(q2[16:64], cd[k], preferred_element_type=F32)
 
-    def distances(pairs):
-        for k, (b, o) in enumerate(pairs):
+    def distances(pairs, first=0):
+        for k, (b, o) in enumerate(pairs, first):
             sqb[k] = jnp.dot(a_ref[b], b_ref[o], preferred_element_type=F32)
 
     def flat(pair, i):
-        out = []
-        for k in range(4):
-            X, Y, Z, o = pair(jnp.asarray(4 * i + k, jnp.int32))
-            out.append((X * 16 + Y * 4 + Z, o))
-        return out
-
-    def phase(pair, lo, hi, last, mask=False):
-        distances(flat(pair, lo))
-        n = hi - lo
+        return [pair(jnp.asarray(i, jnp.int32), k) for k in range(4)]
+
+    def phase(pair, n, last, mask=False):
+        distances(flat(pair, 0))
 
         @pl.loop(0, n)
         def _(i):
             began = lax.div(i + n - 1, n)
-            now = flat(pair, lo + i - began)
-            pending = [(b * began + pb * (1 - began), o * began + po * (1 - began)) for (b, o), (pb, po) in zip(now, last)]
-            reduce_pairs(pending)
+            now = flat(pair, i - began)
+            pending = [(pb + began * (b - pb), po + began * (o - po)) for (b, o), (pb, po) in zip(now, last)]
+            later = flat(pair, i + 1 - lax.div(i + 1, n))
             for k in range(4):
                 keep = None
                 if mask:
-                    p = 4 * (lo + i) + k
-                    same = lax.rem(lax.div(p, 8) - lax.rem(p, 8) + 8, 8)
-                    keep = diff != same * 1000
-                ch, cl, dh, dl = coefs(sqb[k], keep)
+                    off = 4 * odd(i) + k - lax.shift_right_logical(i, 1)
+                    keep = diff != off * off * 1000
+                v = sqb[k]
+                ch, cl, dh, dl = coefs(v[:, 0:128], v[:, 128:256], v[:, 256:384], v[:, 384:512], keep)
+                distances([later[k]], k)
+                reduce_pairs([pending[k]], k)
                 cc[k, 0:128] = ch
                 cc[k, 128:256] = cl
                 cd[k, 0:128] = dh
                 cd[k, 128:256] = dl
-            distances(flat(pair, lo + i + 1 - lax.div(i + 1, n)))
-
-        return [tuple(v) for v in flat(pair, hi - 1)]
+
+        return flat(pair, n - 1)
 
     copies = []
 
@@ -221,7 +214,7 @@
 
     prep(bins_mid(1, 1, 0))
     last = flat(pair_own, 0)
-    last = phase(pair_own, 0, SPLIT, last, mask=True)
+    last = phase(pair_own, 16, last, mask=True)
 
     pl.semaphore_wait(barrier, 9)
     for sx, sy in columns:
@@ -234,8 +227,6 @@
             at(dx, dy),
         )
     near = {p: 4 + i for i, p in enumerate(sides)}
-    if SPLIT < 16:
-        last = phase(pair_own, SPLIT, 16, last, mask=True)
 
     def arrive(which):
         for i in which:
@@ -243,7 +234,7 @@
 
     arrive([near[0, 1], near[0, -1]])
     prep(bins_mid(0, 3, 0))
-    last = phase(pair_y_near, 0, 8, last)
+    last = phase(pair_y_near, 8, last)
     far = {}
     for i, (sx, sy) in enumerate(columns):
         copies[i].wait_recv()
@@ -255,22 +246,22 @@
             far.setdefault(px, []).append(len(copies))
             send(src, reg_ref.at[tx, ty, pl.ds(2, 2)], at(px, py))
     prep(bins_mid(1, 1, 2))
-    last = phase(pair_mid_far, 0, 8, last)
+    last = phase(pair_mid_far, 8, last)
     arrive([near[-1, dy] for dy in (0, 1, -1)])
     prep(bins_side(1, 0))
-    last = phase(pair_x_near(1), 0, 6, last)
+    last = phase(pair_x_near(1), 6, last)
     arrive(far[0])
     prep(bins_mid(0, 3, 2))
-    last = phase(pair_y_far, 0, 4, last)
+    last = phase(pair_y_far, 4, last)
     arrive(far[-1])
     prep(bins_side(1, 2))
-    last = phase(pair_x_far(1), 0, 3, last)
+    last = phase(pair_x_far(1), 3, last)
     arrive([near[1, dy] for dy in (0, 1, -1)])
     prep(bins_side(0, 0))
-    last = phase(pair_x_near(0), 0, 6, last)
+    last = phase(pair_x_near(0), 6, last)
     arrive(far[1])
     prep(bins_side(0, 2))
-    last = phase(pair_x_far(0), 0, 3, last)
+    last = phase(pair_x_far(0), 3, last)
     reduce_pairs(last)
 
     for o in range(8):
@@ -292,9 +283,6 @@
         copy.wait_send()
 
 
-SPLIT = 16
-
-
 def on_device(offsets, forces, counts):
     vel = pl.pallas_call(
         near_kernel,
@@ -310,10 +298,10 @@
             pltpu.VMEM((2, 2, 2, 8, 128), F32),
             pltpu.VMEM((64, 128, 32), BF16),
             pltpu.VMEM((64, 64, 128), BF16),
-            pltpu.VMEM((8, 32, 128), BF16),
+            pltpu.VMEM((8, 32, 512), BF16),
             pltpu.VMEM((4, 256, 128), BF16),
             pltpu.VMEM((4, 256, 128), BF16),
-            pltpu.VMEM((4, 128, 128), F32),
+            pltpu.VMEM((4, 128, 512), F32),
             pltpu.VMEM((8, 16, 128), F32),
             pltpu.VMEM((8, 48, 128), F32),
             pltpu.SemaphoreType.DMA((24,)),

time: 49.2 us -> 47.9 us (0.974)
  Pallas kernels: 47.4 us -> 45.7 us
    pallas_call x1, Pallas kernels: 47.4 us -> 45.7 us  [on_device(): pl.pallas_call(near_kernel, out_shape=jax.ShapeDtypeStruct((3, 8, 128), F...]
where the time goes in v5:
time: 47.9 us; the launch traced here: 47 us
  Pallas kernels  45.7 us (95%)
  local copies, waits for them, and re-layouts  1.31 us (3%)
    pallas_call x1, Pallas kernels, on_device(): pl.pallas_call(near_kernel, out_shape=jax.ShapeDtypeStruct((3, 8, 128), F...  45.7 us
    unnamed x1, local copies, waits for them, and re-layouts  1.31 us

profile of v5, /device:TPU:1, one launch (start us, length us, event | category | flops | bytes accessed | tf_op | source)
XLA Modules:
  0.0 47.0 jit_solution(4801286826405815226)
XLA Ops:
  0.0 45.7 %shard_map.37 = f32[3,8,128]{2,1,0:T(8,128)} custom-call(f32[3,8,128]{2,1,0:T(8,128)} %bitcast.4, f32[3,8,128]{2,1,0:T(8,128)} %bitcast.5, s32[2,2,2]{2,1,0:T(2,128)} %cnt_ref.1), custom_call_target="tpu_custom_call" | custom-call | tf_op jit(solution)/shard_map/pallas_call | solution.py:287
  45.7 1.3 %copy.5 = f32[3,2,2,2,128]{4,3,2,1,0:T(2,128)} copy(f32[3,2,2,2,128]{4,3,2,1,0:T(2,128)} %bitcast.3) | data formatting | bytes 24576

commit v6 on v5

v6 whole, which is shorter than its diff:
```python
import math

import jax
import jax.numpy as jnp
from jax import lax
from jax.experimental import pallas as pl
from jax.experimental.pallas import tpu as pltpu
from jax.sharding import PartitionSpec as P


GAUSS = 4.0 / math.sqrt(math.pi)
NORM = 1.0 / (8.0 * math.pi)
ERFCX = (-6.605853591129529e-05, 0.2835500330769051, 0.2685154202156198, 0.31675806246707194,
         -0.03963002369445217, 0.48597127806071433, -0.4204782835714706, 0.1053890269858883)
F32 = jnp.float32
BF16 = jnp.bfloat16
MESH = pl.DeviceIdType.MESH
FORMS = ((1.0, 0.0), (8.0 * GAUSS, -3.0 * GAUSS), (8.0 * GAUSS, -GAUSS), (-4.0 * math.log2(math.e), 0.0))


def split3(v):
    a = v.astype(BF16).astype(F32)
    r = v - a
    b = r.astype(BF16).astype(F32)
    return a, b, r - b


def coefs(sq, ac, ad, arg, keep=None):
    rs = lax.rsqrt(sq)
    z = sq * rs + 1.0
    t = lax.rsqrt(z * z)
    p = ERFCX[7]
    for q in ERFCX[6::-1]:
        p = p * t + q
    e = rs * p
    g = jnp.exp2(arg)
    if keep is not None:
        g = jnp.where(keep, g, 0.0)
    c = g * (e + ac)
    d = (g * (rs * rs)) * (e - ad)
    ch = c.astype(BF16)
    cl = (c - ch.astype(F32)).astype(BF16)
    dh = d.astype(BF16)
    dl = (d - dh.astype(F32)).astype(BF16)
    return ch, cl, dh, dl


def odd(i):
    return i - 2 * lax.shift_right_logical(i, 1)


def pair_own(i, k):
    return 16 + 16 * odd(i) + (1 + k // 2) * 4 + k % 2, lax.shift_right_logical(i, 1)


def pair_y_near(i, k):
    return (1 + k // 2) * 16 + 12 * odd(lax.shift_right_logical(i, 1)) + k % 2, i


def pair_mid_far(i, k):
    return (1 + k // 2) * 16 + (1 + k % 2) * 4 + 3 - odd(i), i


def pair_y_far(i, k):
    return (1 + k % 2) * 16 + 12 * odd(i) + 3 - k // 2, 2 * i + k // 2


def pair_x_near(side):
    def pair(i, k):
        y = lax.shift_right_logical(11 * i, 5)
        return 48 * side + (i - 2 * y) * 4 + k % 2, 4 * side + 2 * y + k // 2
    return pair


def pair_x_far(side):
    def pair(i, k):
        return 48 * side + (k // 2 + i) * 4 + 3 - k % 2, jnp.int32(0) + 4 * side + k
    return pair


def bins_mid(y0, ystep, z0):
    def new(n):
        return 1 + n // 4, y0 + ystep * ((n // 2) % 2), z0 + n % 2
    return new


def bins_side(side, z0):
    def new(n):
        return 3 * side, n // 2, z0 + n % 2
    return new


def machinery(tile_of, a_ref, q_ref, b_ref, cc, cd, sqb, acc_c, acc_d):
    sub = lax.broadcasted_iota(jnp.int32, (128, 128), 0)
    diff = lax.broadcasted_iota(jnp.int32, (128, 128), 1) - sub
    one = jnp.ones((1, 128), F32)
    zero = jnp.zeros((1, 128), F32)
    cc[...] = jnp.zeros((4, 256, 128), F32).astype(BF16)
    cd[...] = jnp.zeros((4, 256, 128), F32).astype(BF16)

    def target(o):
        tile = tile_of(1 + o // 4, 1 + (o // 2) % 2, o % 2)
        x = tile[4:5] + float(o // 4 - 1)
        y = tile[5:6] + float((o // 2) % 2 - 1)
        z = tile[6:7] + float(o % 2 - 1)
        return tile, x, y, z

    def targets():
        for o in range(8):
            tile, x, y, z = target(o)
            m = x * x + y * y + z * z + 0.01
            for k, (scale, extra) in enumerate(FORMS):
                t1, t2, t3 = split3(scale * jnp.concatenate([x, y, z, one], axis=0))
                m1, m2, m3 = split3(scale * m + extra)
                b_ref[o, :, 128 * k:128 * (k + 1)] = jnp.concatenate(
                    [t1, t2, t3, t1, t2, t1, m1, m2, m3, zero, zero, zero, zero, zero], axis=0
                ).astype(BF16)

    def prep(new):
        for k in range(8):
            X, Y, Z = new(k)
            b = X * 16 + Y * 4 + Z
            tile = tile_of(X, Y, Z)
            f = tile[0:3]
            x = tile[4:5] + float(X - 2)
            y = tile[5:6] + float(Y - 2)
            z = tile[6:7] + float(Z - 1 - 4 * (Z // 3))
            n = x * x + y * y + z * z
            r1, r2, r3 = split3(jnp.concatenate([-2.0 * x, -2.0 * y, -2.0 * z, n], axis=0))
            feat = jnp.concatenate([r1, r1, r1, r2, r2, r3, jnp.ones((8, 128), F32)], axis=0)
            a_ref[b] = feat.T.astype(BF16)
            w = x * f[0:1] + y * f[1:2] + z * f[2:3]
            g4 = jnp.concatenate([f, w], axis=0)
            a3 = split3(jnp.concatenate([g4, x * g4], axis=0))
            b3 = split3(jnp.concatenate([y * g4, z * g4], axis=0))
            q = jnp.concatenate([a3[0], a3[1], a3[0], b3[0], a3[1], b3[1], a3[2], b3[2]], axis=0)
            q_ref[b] = q.astype(BF16)

    def reduce_pairs(pairs, first=0):
        for k, (b, o) in enumerate(pairs, first):
            q = q_ref[b]
            q2 = jnp.concatenate([q, q], axis=1)
            acc_c[o] = acc_c[o] + jnp.dot(q2[0:16], cc[k], preferred_element_type=F32)
            acc_d[o] = acc_d[o] + jnp.dot(q2[16:64], cd[k], preferred_element_type=F32)

    def distances(pairs, first=0):
        for k, (b, o) in enumerate(pairs, first):
            sqb[k] = jnp.dot(a_ref[b], b_ref[o], preferred_element_type=F32)

    def flat(pair, i):
        return [pair(jnp.asarray(i, jnp.int32), k) for k in range(4)]

    def phase(pair, n, last, mask=False, opening=True, following=None):
        if opening:
            distances(flat(pair, 0))

        @pl.loop(0, n)
        def _(i):
            began = lax.div(i + n - 1, n)
            now = flat(pair, i - began)
            pending = [(pb + began * (b - pb), po + began * (o - po)) for (b, o), (pb, po) in zip(now, last)]
            ended = lax.div(i + 1, n)
            later = flat(pair, i + 1 - ended)
            if following is not None:
                first = flat(following, 0)
                later = [(b + ended * (nb - b), o + ended * (no - o)) for (b, o), (nb, no) in zip(later, first)]
            for k in range(4):
                keep = None
                if mask:
                    off = 4 * odd(i) + k - lax.shift_right_logical(i, 1)
                    keep = diff != off * off * 1000
                v = sqb[k]
                ch, cl, dh, dl = coefs(v[:, 0:128], v[:, 128:256], v[:, 256:384], v[:, 384:512], keep)
                distances([later[k]], k)
                reduce_pairs([pending[k]], k)
                cc[k, 0:128] = ch
                cc[k, 128:256] = cl
                cd[k, 0:128] = dh
                cd[k, 128:256] = dl

        return flat(pair, n - 1)

    return target, targets, prep, reduce_pairs, flat, phase


def own_kernel(off_ref, frc_ref, cnt_ref, mid_ref, acc_c, acc_d, send_ref, a_ref, q_ref, b_ref, cc, cd, sqb, send_sems, recv_sems):
    ix = lax.axis_index("gx")
    iy = lax.axis_index("gy")
    ih = lax.axis_index("ha")
    ny = lax.axis_size("gy")
    partner = (ix, iy, 1 - ih)
    beside = {dy: (ix, lax.rem(iy + dy + ny, ny), ih) for dy in (1, -1)}
    barrier = pltpu.get_barrier_semaphore()
    for device in (partner, beside[1], beside[-1]):
        pl.semaphore_signal(barrier, inc=1, device_id=device, device_id_type=MESH)

    lane = lax.broadcasted_iota(jnp.int32, (1, 128), 1)
    for b in range(8):
        bx, by, bz = b // 4, (b // 2) % 2, b % 2
        live = (lane < cnt_ref[bx, by, bz]).astype(F32)
        rows = [frc_ref[r, b:b + 1] * live for r in range(3)] + [live]
        rows += [off_ref[r, b:b + 1] for r in range(3)] + [jnp.zeros((1, 128), F32)]
        tile = jnp.concatenate(rows, axis=0)
        send_ref[bx, by, bz] = tile
        mid_ref[bx, 1 + by, bz] = tile
    acc_c[...] = jnp.zeros_like(acc_c)
    acc_d[...] = jnp.zeros_like(acc_d)
    target, targets, prep, reduce_pairs, flat, phase = machinery(
        lambda X, Y, Z: mid_ref[X - 1, Y, Z], a_ref, q_ref, b_ref, cc, cd, sqb, acc_c, acc_d
    )
    copies = []

    def send(src, dst, device):
        i = len(copies)
        copy = pltpu.make_async_remote_copy(
            src_ref=src, dst_ref=dst, send_sem=send_sems.at[i], recv_sem=recv_sems.at[i],
            device_id=device, device_id_type=MESH,
        )
        copy.start()
        copies.append(copy)

    targets()
    prep(bins_mid(1, 1, 0))
    pl.semaphore_wait(barrier, 3)
    columns = [(sx, sy) for sx in range(2) for sy in range(2)]
    for sx, sy in columns:
        send(send_ref.at[sx, sy], mid_ref.at[sx, 1 + sy, pl.ds(2, 2)], partner)
    for dy in (1, -1):
        for sx in range(2):
            send(send_ref.at[sx, (1 + dy) // 2], mid_ref.at[sx, (3 - 3 * dy) // 2, pl.ds(0, 2)], beside[dy])
    last = flat(pair_own, 0)
    last = phase(pair_own, 16, last, mask=True)
    for i, (sx, sy) in enumerate(columns):
        copies[i].wait_recv()
        dy = 2 * sy - 1
        send(mid_ref.at[sx, 1 + sy, pl.ds(2, 2)], mid_ref.at[sx, (3 - 3 * dy) // 2, pl.ds(2, 2)], beside[dy])
    reduce_pairs(last)
    for copy in copies[4:]:
        copy.wait_recv()
    for copy in copies:
        copy.wait_send()


def near_kernel(mid_ref, acc_c_in, acc_d_in, out_ref, side_ref, acc_c, acc_d, a_ref, q_ref, b_ref, cc, cd, sqb, send_sems, recv_sems):
    ix = lax.axis_index("gx")
    iy = lax.axis_index("gy")
    ih = lax.axis_index("ha")
    nx = lax.axis_size("gx")
    up = (lax.rem(ix + 1, nx), iy, ih)
    down = (lax.rem(ix + nx - 1, nx), iy, ih)
    barrier = pltpu.get_barrier_semaphore()
    for device in (up, down):
        pl.semaphore_signal(barrier, inc=1, device_id=device, device_id_type=MESH)

    def copy_of(i, plane, side, device):
        return pltpu.make_async_remote_copy(
            src_ref=mid_ref.at[plane], dst_ref=side_ref.at[side], send_sem=send_sems.at[i], recv_sem=recv_sems.at[i],
            device_id=device, device_id_type=MESH,
        )

    to_up = copy_of(0, 1, 0, up)
    to_down = copy_of(1, 0, 1, down)

    def exchange():
        pl.semaphore_wait(barrier, 2)
        to_up.start()
        to_down.start()

    first = lax.rem(ix, 8)

    @pl.when(first > 0)
    def _():
        exchange()

    acc_c[...] = acc_c_in[...]
    acc_d[...] = acc_d_in[...]

    def tile_of(X, Y, Z):
        return mid_ref[X - 1, Y, Z] if X in (1, 2) else side_ref[X // 3, Y, Z]

    target, targets, prep, reduce_pairs, flat, phase = machinery(
        tile_of, a_ref, q_ref, b_ref, cc, cd, sqb, acc_c, acc_d
    )
    targets()
    for new in (bins_mid(0, 3, 0), bins_mid(1, 1, 2), bins_mid(0, 3, 2)):
        prep(new)
    last = phase(pair_y_near, 8, flat(pair_y_near, 0), following=pair_mid_far)
    last = phase(pair_mid_far, 8, last, opening=False, following=pair_y_far)
    last = phase(pair_y_far, 4, last, opening=False)
    to_down.wait_recv()
    prep(bins_side(1, 0))
    prep(bins_side(1, 2))
    last = phase(pair_x_near(1), 6, last, following=pair_x_far(1))
    last = phase(pair_x_far(1), 3, last, opening=False)

    @pl.when(first == 0)
    def _():
        exchange()

    to_up.wait_recv()
    prep(bins_side(0, 0))
    prep(bins_side(0, 2))
    last = phase(pair_x_near(0), 6, last, following=pair_x_far(0))
    last = phase(pair_x_far(0), 3, last, opening=False)
    reduce_pairs(last)

    for o in range(8):
        tile, x, y, z = target(o)
        tp = [x, y, z]
        cv = acc_c[o, 8:11] + acc_c[o, 0:3]
        dq = (acc_d[o, 32:48] + acc_d[o, 16:32]) + acc_d[o, 0:16]
        live = tile[3:4] * NORM
        xf = (x * dq[0:1] + y * dq[1:2] + z * dq[2:3]) - dq[3:4]
        for a in range(3):
            i = 4 + 4 * a
            v = cv[a:a + 1] + tp[a] * xf
            v = v - ((x * dq[i:i + 1] + y * dq[i + 1:i + 2] + z * dq[i + 2:i + 3]) - dq[i + 3:i + 4])
            out_ref[a, o:o + 1] = v * live
    to_up.wait_send()
    to_down.wait_send()


WORK = [
    pltpu.VMEM((64, 128, 32), BF16),
    pltpu.VMEM((64, 64, 128), BF16),
    pltpu.VMEM((8, 32, 512), BF16),
    pltpu.VMEM((4, 256, 128), BF16),
    pltpu.VMEM((4, 256, 128), BF16),
    pltpu.VMEM((4, 128, 512), F32),
]
SUMS = [(8, 16, 128), (8, 48, 128)]


def on_device(offsets, forces, counts):
    vmem = pl.BlockSpec(memory_space=pltpu.VMEM)
    mid, sum_c, sum_d = pl.pallas_call(
        own_kernel,
        out_shape=[jax.ShapeDtypeStruct(s, F32) for s in [(2, 4, 4, 8, 128)] + SUMS],
        in_specs=[vmem, vmem, pl.BlockSpec(memory_space=pltpu.SMEM)],
        out_specs=[vmem] * 3,
        scratch_shapes=[pltpu.VMEM((2, 2, 2, 8, 128), F32)] + WORK + [pltpu.SemaphoreType.DMA((12,))] * 2,
        compiler_params=pltpu.CompilerParams(collective_id=0, has_side_effects=True),
    )(offsets.reshape(3, 8, 128), forces.reshape(3, 8, 128), counts)
    vel = pl.pallas_call(
        near_kernel,
        out_shape=jax.ShapeDtypeStruct((3, 8, 128), F32),
        in_specs=[vmem] * 3,
        out_specs=vmem,
        scratch_shapes=[pltpu.VMEM((2, 4, 4, 8, 128), F32)] + [pltpu.VMEM(s, F32) for s in SUMS] + WORK
        + [pltpu.SemaphoreType.DMA((2,))] * 2,
        compiler_params=pltpu.CompilerParams(collective_id=1, has_side_effects=True),
    )(mid, sum_c, sum_d)
    return vel.reshape(3, 2, 2, 2, 128)


def solution(mesh):
    spec = P(None, "gx", "gy", "ha", None)
    return jax.shard_map(
        on_device, mesh=mesh, in_specs=(spec, spec, P("gx", "gy", "ha")), out_specs=spec, check_vma=False
    )
```

time: 47.9 us -> 49.4 us (1.031)
  the two profiles are of different devices: /device:TPU:1 before, /device:TPU:128 now
where the time goes in v6:
time: 49.4 us; the launch traced here: 49 us
  Pallas kernels  47.7 us (97%)
  local copies, waits for them, and re-layouts  1.31 us (3%)
    pallas_call x1, Pallas kernels, on_device(): pl.pallas_call(near_kernel, out_shape=jax.ShapeDtypeStruct((3, 8, 128), F...  28.2 us
    pallas_call x1, Pallas kernels, on_device(): pl.pallas_call(own_kernel, out_shape=[jax.ShapeDtypeStruct(s, F32) for s...  19.5 us
    unnamed x1, local copies, waits for them, and re-layouts  1.31 us

profile of v6, /device:TPU:128, one launch (start us, length us, event | category | flops | bytes accessed | tf_op | source)
XLA Modules:
  0.0 49.0 jit_solution(544763271350579825)
XLA Ops:
  0.0 19.5 %shard_map.37 = (f32[2,4,4,8,128]{4,3,2,1,0:T(8,128)}, f32[8,16,128]{2,1,0:T(8,128)}, f32[8,48,128]{2,1,0:T(8,128)}) custom-call(f32[3,8,128]{2,1,0:T(8,128)} %bitcast.4, f32[3,8,128]{2,1,0:T(8,128)} %bitcast.5, s32[2,2,2]{2,1,0:T(2,128)} %cnt_ref.1), custom_call_target="tpu_custom_call" | custom-call | tf_op jit(solution)/shard_map/pallas_call | solution.py:336
  19.5 28.2 %shard_map.38 = f32[3,8,128]{2,1,0:T(8,128)} custom-call(f32[2,4,4,8,128]{4,3,2,1,0:T(8,128)} %get-tuple-element.8.mid_ref, f32[8,16,128]{2,1,0:T(8,128)} %get-tuple-element.9.acc_c_in, f32[8,48,128]{2,1,0:T(8,128)} %get-tuple-element.10.acc_d_in), custom_call_target="tpu_custom_call" | custom-call | tf_op jit(solution)/shard_map/pallas_call | solution.py:344
  47.7 1.3 %copy.5 = f32[3,2,2,2,128]{4,3,2,1,0:T(2,128)} copy(f32[3,2,2,2,128]{4,3,2,1,0:T(2,128)} %bitcast.3) | data formatting | bytes 24576

commit v7 on v6

--- a/solution.py
+++ b/solution.py
@@ -150,24 +150,24 @@
     def flat(pair, i):
         return [pair(jnp.asarray(i, jnp.int32), k) for k in range(4)]
 
-    def phase(pair, n, last, mask=False, opening=True, following=None):
+    def phase(pair, n, last, mask=False, opening=True, following=None, start=0):
         if opening:
-            distances(flat(pair, 0))
+            distances(flat(pair, start))
 
         @pl.loop(0, n)
         def _(i):
             began = lax.div(i + n - 1, n)
-            now = flat(pair, i - began)
+            now = flat(pair, start + i - began)
             pending = [(pb + began * (b - pb), po + began * (o - po)) for (b, o), (pb, po) in zip(now, last)]
             ended = lax.div(i + 1, n)
-            later = flat(pair, i + 1 - ended)
+            later = flat(pair, start + i + 1 - ended)
             if following is not None:
                 first = flat(following, 0)
                 later = [(b + ended * (nb - b), o + ended * (no - o)) for (b, o), (nb, no) in zip(later, first)]
             for k in range(4):
                 keep = None
                 if mask:
-                    off = 4 * odd(i) + k - lax.shift_right_logical(i, 1)
+                    off = 4 * odd(start + i) + k - lax.shift_right_logical(start + i, 1)
                     keep = diff != off * off * 1000
                 v = sqb[k]
                 ch, cl, dh, dl = coefs(v[:, 0:128], v[:, 128:256], v[:, 256:384], v[:, 384:512], keep)
@@ -178,7 +178,7 @@
                 cd[k, 0:128] = dh
                 cd[k, 128:256] = dl
 
-        return flat(pair, n - 1)
+        return flat(pair, start + n - 1)
 
     return target, targets, prep, reduce_pairs, flat, phase
 
@@ -229,11 +229,12 @@
         for sx in range(2):
             send(send_ref.at[sx, (1 + dy) // 2], mid_ref.at[sx, (3 - 3 * dy) // 2, pl.ds(0, 2)], beside[dy])
     last = flat(pair_own, 0)
-    last = phase(pair_own, 16, last, mask=True)
+    last = phase(pair_own, 10, last, mask=True)
     for i, (sx, sy) in enumerate(columns):
         copies[i].wait_recv()
         dy = 2 * sy - 1
         send(mid_ref.at[sx, 1 + sy, pl.ds(2, 2)], mid_ref.at[sx, (3 - 3 * dy) // 2, pl.ds(2, 2)], beside[dy])
+    last = phase(pair_own, 6, last, mask=True, start=10)
     reduce_pairs(last)
     for copy in copies[4:]:
         copy.wait_recv()
@@ -286,16 +287,17 @@
         prep(new)
     last = phase(pair_y_near, 8, flat(pair_y_near, 0), following=pair_mid_far)
     last = phase(pair_mid_far, 8, last, opening=False, following=pair_y_far)
+
+    @pl.when(first == 0)
+    def _():
+        exchange()
+
     last = phase(pair_y_far, 4, last, opening=False)
     to_down.wait_recv()
     prep(bins_side(1, 0))
     prep(bins_side(1, 2))
     last = phase(pair_x_near(1), 6, last, following=pair_x_far(1))
     last = phase(pair_x_far(1), 3, last, opening=False)
-
-    @pl.when(first == 0)
-    def _():
-        exchange()
 
     to_up.wait_recv()
     prep(bins_side(0, 0))

time: 49.4 us -> 47.7 us (0.966)
  the two profiles are of different devices: /device:TPU:128 before, /device:TPU:1 now
where the time goes in v7:
time: 47.7 us; the launch traced here: 47.3 us
  Pallas kernels  46 us (96%)
  local copies, waits for them, and re-layouts  1.31 us (3%)
    pallas_call x1, Pallas kernels, on_device(): pl.pallas_call(own_kernel, out_shape=[jax.ShapeDtypeStruct(s, F32) for s...  25.2 us
    pallas_call x1, Pallas kernels, on_device(): pl.pallas_call(near_kernel, out_shape=jax.ShapeDtypeStruct((3, 8, 128), F...  20.8 us
    unnamed x1, local copies, waits for them, and re-layouts  1.31 us

profile of v7, /device:TPU:1, one launch (start us, length us, event | category | flops | bytes accessed | tf_op | source)
XLA Modules:
  0.0 47.3 jit_solution(16731961882529205932)
XLA Ops:
  0.0 25.2 %shard_map.37 = (f32[2,4,4,8,128]{4,3,2,1,0:T(8,128)}, f32[8,16,128]{2,1,0:T(8,128)}, f32[8,48,128]{2,1,0:T(8,128)}) custom-call(f32[3,8,128]{2,1,0:T(8,128)} %bitcast.4, f32[3,8,128]{2,1,0:T(8,128)} %bitcast.5, s32[2,2,2]{2,1,0:T(2,128)} %cnt_ref.1), custom_call_target="tpu_custom_call" | custom-call | tf_op jit(solution)/shard_map/pallas_call | solution.py:338
  25.2 20.8 %shard_map.38 = f32[3,8,128]{2,1,0:T(8,128)} custom-call(f32[2,4,4,8,128]{4,3,2,1,0:T(8,128)} %get-tuple-element.8.mid_ref, f32[8,16,128]{2,1,0:T(8,128)} %get-tuple-element.9.acc_c_in, f32[8,48,128]{2,1,0:T(8,128)} %get-tuple-element.10.acc_d_in), custom_call_target="tpu_custom_call" | custom-call | tf_op jit(solution)/shard_map/pallas_call | solution.py:346
  46.0 1.3 %copy.5 = f32[3,2,2,2,128]{4,3,2,1,0:T(2,128)} copy(f32[3,2,2,2,128]{4,3,2,1,0:T(2,128)} %bitcast.3) | data formatting | bytes 24576

commit v8 on v7

--- a/solution.py
+++ b/solution.py
@@ -97,6 +97,7 @@
     zero = jnp.zeros((1, 128), F32)
     cc[...] = jnp.zeros((4, 256, 128), F32).astype(BF16)
     cd[...] = jnp.zeros((4, 256, 128), F32).astype(BF16)
+    q_ref[64] = jnp.zeros((64, 128), F32).astype(BF16)
 
     def target(o):
         tile = tile_of(1 + o // 4, 1 + (o // 2) % 2, o % 2)
@@ -183,6 +184,10 @@
     return target, targets, prep, reduce_pairs, flat, phase
 
 
+def lateness(ix, iy, ny):
+    return lax.rem(ix, 8) * 2 + lax.div(ny - iy, ny)
+
+
 def own_kernel(off_ref, frc_ref, cnt_ref, mid_ref, acc_c, acc_d, send_ref, a_ref, q_ref, b_ref, cc, cd, sqb, send_sems, recv_sems):
     ix = lax.axis_index("gx")
     iy = lax.axis_index("gy")
@@ -221,6 +226,12 @@
 
     targets()
     prep(bins_mid(1, 1, 0))
+    late = lateness(ix, iy, ny)
+
+    @pl.when(late == 0)
+    def _():
+        reduce_pairs(phase(pair_own, 16, NONE, mask=True))
+
     pl.semaphore_wait(barrier, 3)
     columns = [(sx, sy) for sx in range(2) for sy in range(2)]
     for sx, sy in columns:
@@ -228,14 +239,25 @@
     for dy in (1, -1):
         for sx in range(2):
             send(send_ref.at[sx, (1 + dy) // 2], mid_ref.at[sx, (3 - 3 * dy) // 2, pl.ds(0, 2)], beside[dy])
-    last = flat(pair_own, 0)
-    last = phase(pair_own, 10, last, mask=True)
+
+    @pl.when(late > 0)
+    def _():
+        reduce_pairs(phase(pair_own, 10, NONE, mask=True))
+
     for i, (sx, sy) in enumerate(columns):
         copies[i].wait_recv()
         dy = 2 * sy - 1
         send(mid_ref.at[sx, 1 + sy, pl.ds(2, 2)], mid_ref.at[sx, (3 - 3 * dy) // 2, pl.ds(2, 2)], beside[dy])
-    last = phase(pair_own, 6, last, mask=True, start=10)
-    reduce_pairs(last)
+
+    @pl.when(late > 0)
+    def _():
+        reduce_pairs(phase(pair_own, 6, NONE, mask=True, start=10))
+
+    @pl.when(late == 0)
+    def _():
+        prep(bins_mid(1, 1, 2))
+        reduce_pairs(phase(pair_mid_far, 8, NONE))
+
     for copy in copies[4:]:
         copy.wait_recv()
     for copy in copies:
@@ -247,6 +269,8 @@
     iy = lax.axis_index("gy")
     ih = lax.axis_index("ha")
     nx = lax.axis_size("gx")
+    ny = lax.axis_size("gy")
+    late = lateness(ix, iy, ny)
     up = (lax.rem(ix + 1, nx), iy, ih)
     down = (lax.rem(ix + nx - 1, nx), iy, ih)
     barrier = pltpu.get_barrier_semaphore()
@@ -267,9 +291,8 @@
         to_up.start()
         to_down.start()
 
-    first = lax.rem(ix, 8)
-
-    @pl.when(first > 0)
+
+    @pl.when(late > 1)
     def _():
         exchange()
 
@@ -283,21 +306,30 @@
         tile_of, a_ref, q_ref, b_ref, cc, cd, sqb, acc_c, acc_d
     )
     targets()
-    for new in (bins_mid(0, 3, 0), bins_mid(1, 1, 2), bins_mid(0, 3, 2)):
+    for new in (bins_mid(0, 3, 0), bins_mid(0, 3, 2)):
         prep(new)
-    last = phase(pair_y_near, 8, flat(pair_y_near, 0), following=pair_mid_far)
-    last = phase(pair_mid_far, 8, last, opening=False, following=pair_y_far)
-
-    @pl.when(first == 0)
+    reduce_pairs(phase(pair_y_near, 8, NONE))
+
+    @pl.when(late > 0)
+    def _():
+        prep(bins_mid(1, 1, 2))
+        reduce_pairs(phase(pair_mid_far, 8, NONE))
+
+    @pl.when(late == 1)
     def _():
         exchange()
 
-    last = phase(pair_y_far, 4, last, opening=False)
+    last = phase(pair_y_far, 4, NONE)
     to_down.wait_recv()
     prep(bins_side(1, 0))
     prep(bins_side(1, 2))
     last = phase(pair_x_near(1), 6, last, following=pair_x_far(1))
     last = phase(pair_x_far(1), 3, last, opening=False)
+
+    @pl.when(late == 0)
+    def _():
+        exchange()
+
 
     to_up.wait_recv()
     prep(bins_side(0, 0))
@@ -324,12 +356,13 @@
 
 WORK = [
     pltpu.VMEM((64, 128, 32), BF16),
-    pltpu.VMEM((64, 64, 128), BF16),
+    pltpu.VMEM((65, 64, 128), BF16),
     pltpu.VMEM((8, 32, 512), BF16),
     pltpu.VMEM((4, 256, 128), BF16),
     pltpu.VMEM((4, 256, 128), BF16),
     pltpu.VMEM((4, 128, 512), F32),
 ]
+NONE = [(64, 0)] * 4
 SUMS = [(8, 16, 128), (8, 48, 128)]
 
 

time: 47.7 us -> 47.1 us (0.987)
  the two profiles are of different devices: /device:TPU:1 before, /device:TPU:128 now
where the time goes in v8:
time: 47.1 us; the launch traced here: 46.8 us
  Pallas kernels  45.5 us (97%)
  local copies, waits for them, and re-layouts  1.31 us (3%)
    pallas_call x1, Pallas kernels, on_device(): pl.pallas_call(near_kernel, out_shape=jax.ShapeDtypeStruct((3, 8, 128), F...  28.4 us
    pallas_call x1, Pallas kernels, on_device(): pl.pallas_call(own_kernel, out_shape=[jax.ShapeDtypeStruct(s, F32) for s...  17 us
    unnamed x1, local copies, waits for them, and re-layouts  1.31 us

profile of v8, /device:TPU:128, one launch (start us, length us, event | category | flops | bytes accessed | tf_op | source)
XLA Modules:
  0.0 46.8 jit_solution(3216876186265261208)
XLA Ops:
  0.0 17.0 %shard_map.37 = (f32[2,4,4,8,128]{4,3,2,1,0:T(8,128)}, f32[8,16,128]{2,1,0:T(8,128)}, f32[8,48,128]{2,1,0:T(8,128)}) custom-call(f32[3,8,128]{2,1,0:T(8,128)} %bitcast.4, f32[3,8,128]{2,1,0:T(8,128)} %bitcast.5, s32[2,2,2]{2,1,0:T(2,128)} %cnt_ref.1), custom_call_target="tpu_custom_call" | custom-call | tf_op jit(solution)/shard_map/pallas_call | solution.py:371
  17.0 28.4 %shard_map.38 = f32[3,8,128]{2,1,0:T(8,128)} custom-call(f32[2,4,4,8,128]{4,3,2,1,0:T(8,128)} %get-tuple-element.8.mid_ref, f32[8,16,128]{2,1,0:T(8,128)} %get-tuple-element.9.acc_c_in, f32[8,48,128]{2,1,0:T(8,128)} %get-tuple-element.10.acc_d_in), custom_call_target="tpu_custom_call" | custom-call | tf_op jit(solution)/shard_map/pallas_call | solution.py:379
  45.5 1.3 %copy.5 = f32[3,2,2,2,128]{4,3,2,1,0:T(2,128)} copy(f32[3,2,2,2,128]{4,3,2,1,0:T(2,128)} %bitcast.3) | data formatting | bytes 24576

commit v9 on v8

--- a/solution.py
+++ b/solution.py
@@ -343,7 +343,7 @@
         tp = [x, y, z]
         cv = acc_c[o, 8:11] + acc_c[o, 0:3]
         dq = (acc_d[o, 32:48] + acc_d[o, 16:32]) + acc_d[o, 0:16]
-        live = tile[3:4] * NORM
+        live = tile[3:4]
         xf = (x * dq[0:1] + y * dq[1:2] + z * dq[2:3]) - dq[3:4]
         for a in range(3):
             i = 4 + 4 * a
@@ -385,7 +385,7 @@
         + [pltpu.SemaphoreType.DMA((2,))] * 2,
         compiler_params=pltpu.CompilerParams(collective_id=1, has_side_effects=True),
     )(mid, sum_c, sum_d)
-    return vel.reshape(3, 2, 2, 2, 128)
+    return vel.reshape(3, 2, 2, 2, 128) * NORM
 
 
 def solution(mesh):

time: 47.1 us -> 47.1 us (level)
  other arithmetic: 0 us -> 1.31 us
  local copies, waits for them, and re-layouts: 1.31 us -> 0 us
    mul x0 -> x1, other arithmetic: none -> 1.31 us  [on_device(): return vel.reshape(3, 2, 2, 2, 128) * NORM]
    unnamed x1 -> x0, local copies, waits for them, and re-layouts: 1.31 us -> none
where the time goes in v9:
time: 47.1 us; the launch traced here: 46.8 us
  Pallas kernels  45.5 us (97%)
  other arithmetic  1.31 us (3%)
    pallas_call x1, Pallas kernels, on_device(): pl.pallas_call(near_kernel, out_shape=jax.ShapeDtypeStruct((3, 8, 128), F...  28.4 us
    pallas_call x1, Pallas kernels, on_device(): pl.pallas_call(own_kernel, out_shape=[jax.ShapeDtypeStruct(s, F32) for s...  17 us
    mul x1, other arithmetic, on_device(): return vel.reshape(3, 2, 2, 2, 128) * NORM  1.31 us

profile of v9, /device:TPU:128, one launch (start us, length us, event | category | flops | bytes accessed | tf_op | source)
XLA Modules:
  0.0 46.8 jit_solution(9684223800654110793)
XLA Ops:
  0.0 17.0 %shard_map.37 = (f32[2,4,4,8,128]{4,3,2,1,0:T(8,128)}, f32[8,16,128]{2,1,0:T(8,128)}, f32[8,48,128]{2,1,0:T(8,128)}) custom-call(f32[3,8,128]{2,1,0:T(8,128)} %bitcast.3, f32[3,8,128]{2,1,0:T(8,128)} %bitcast.4, s32[2,2,2]{2,1,0:T(2,128)} %cnt_ref.1), custom_call_target="tpu_custom_call" | custom-call | tf_op jit(solution)/shard_map/pallas_call | solution.py:371
  17.0 28.4 %shard_map.38 = f32[3,8,128]{2,1,0:T(8,128)} custom-call(f32[2,4,4,8,128]{4,3,2,1,0:T(8,128)} %get-tuple-element.8.mid_ref, f32[8,16,128]{2,1,0:T(8,128)} %get-tuple-element.9.acc_c_in, f32[8,48,128]{2,1,0:T(8,128)} %get-tuple-element.10.acc_d_in), custom_call_target="tpu_custom_call" | custom-call | tf_op jit(solution)/shard_map/pallas_call | solution.py:379
  45.5 1.3 %broadcast_multiply_fusion = f32[3,8,128]{2,1,0:T(8,128)} fusion(f32[3,8,128]{2,1,0:T(8,128)} %shard_map.38), kind=kLoop, calls=%fused_computation | loop fusion | flops 3072 | bytes 24576 | tf_op jit(solution)/shard_map/mul | solution.py:388
